TPU v7x, 256 devices: a whole 4x4x8 slice. The times are simulated.
256 devices in a mesh: gy: 4 (over x), gx: 4 (over z_hi), ga: 16 (over y, z_lo, core).
Axes of the slice: x: 4, y: 4, z: 8 (z_hi: 4, z_lo: 2; z = z_hi * 2 + z_lo), core: 2. Of those that a mesh axis runs over, the one named last changes fastest.
Arguments:
- volume: bfloat16 [16, 56, 56, 7, 768], P('ga', 'gy', 'gx'), may hold values from -6 to 6
- affinity: bfloat16 [16, 3, 56, 56, 7], P('ga', None, 'gy', 'gx'), may hold values from 0 to 1
- window_dest: int32 [16, 4, 4, 4], P('ga', 'gy', 'gx'), may hold values from 0 to 16, as said below
- qkv_weight: bfloat16 [768, 1152], replicated
- proj_weight: bfloat16 [384, 768], replicated, may hold values from -0.3125 to 0.3125
- head_weight: bfloat16 [768, 3], replicated, may hold values from -0.21875 to 0.21875
Outputs:
- grad_volume: bfloat16 [16, 56, 56, 7, 768], P('ga', 'gy', 'gx')
- grad_qkv: float32 [768, 1152], P('ga')
- grad_proj: float32 [384, 768], P(None, 'ga')
Inputs may be any that keep to these rules, and one draw needn't show every extreme that they name: `window_dest`: 16 marks an empty window; any other value names the device along ga, with the same gy and gx, that computes the window: the device itself or one of the min(2, 15) devices after it, cyclically (index plus 1, plus 2, modulo 16). Every device computes exactly 2 live windows, receives at most 1 from any one device, and in every group some device has 4 live windows (all of its windows), keeps 2 of them and sends 1 to each of the 2 devices after it along ga.
All inputs are finite; a program needn't handle non-finite values.
Results may differ from a plain program's by a relative error of at most 0.0065.
The roundings to bfloat16 on the way count: a program that leaves them out, or rounds other values in their place, can miss the bound.
Values may be sent and summed in bfloat16 or wider, within the bound.
No kernel may reach another device: no remote copies, remote signals or barrier semaphores. Data moves between devices by JAX's collectives and lax.ppermute only.
A program may use at most 128 MiB of HBM per device.

v0:
```python
import jax
import jax.numpy as jnp
from jax import lax
from jax.sharding import PartitionSpec as P

HEAD = 32
WIN = 7
HOPS = 2


LOSS_SCALE = 32.0
EPSILON = 1e-05


def passed_along(block, axis, distance):
    devices = range(lax.axis_size(axis))
    route = [((i - distance) % len(devices), i) for i in devices]
    return lax.ppermute(block, axis, route)


def for_sending(value):
    return jax.tree.map(lambda a: a.astype(jnp.bfloat16) if a.dtype == jnp.float32 else a, value)


def window_grads(tokens, target, region, qkv_weight, proj_weight, head_weight):
    inner_width = proj_weight.shape[0]
    head_count = inner_width // HEAD
    token_count = tokens.shape[0]
    score_scale = HEAD ** (-0.5)
    floated = tokens.astype(jnp.float32)
    mean_row = jnp.mean(floated, axis=-1, keepdims=True)
    centred = floated - mean_row
    variance = jnp.mean(centred * centred, axis=-1, keepdims=True)
    inv_std = lax.rsqrt(variance + EPSILON)
    unit_rows = centred * inv_std
    normed = unit_rows.astype(jnp.bfloat16)
    projected = jnp.dot(normed, qkv_weight, preferred_element_type=jnp.float32).astype(jnp.bfloat16)
    queries = projected[:, :inner_width].reshape(token_count, head_count, HEAD)
    key_rows = projected[:, inner_width : 2 * inner_width].reshape(token_count, head_count, HEAD)
    values = projected[:, 2 * inner_width :].reshape(token_count, head_count, HEAD)
    scores = (
        jnp.einsum("qhd,khd->hqk", queries, key_rows, preferred_element_type=jnp.float32)
        * score_scale
    )
    allowed = region[:, None] == region[None, :]
    scores = jnp.where(allowed[None], scores, jnp.float32(-1e30))
    row_max = jnp.max(scores, axis=-1, keepdims=True)
    exponent = jnp.exp(scores - row_max)
    attend = exponent / jnp.sum(exponent, axis=-1, keepdims=True)
    attend_low = attend.astype(jnp.bfloat16)
    mixed = (
        jnp.einsum("hqk,khd->qhd", attend_low, values, preferred_element_type=jnp.float32)
        .reshape(token_count, inner_width)
        .astype(jnp.bfloat16)
    )
    output = floated + jnp.dot(mixed, proj_weight, preferred_element_type=jnp.float32)
    output_low = output.astype(jnp.bfloat16)
    logits = jnp.dot(output_low, head_weight, preferred_element_type=jnp.float32)
    logit_grad = LOSS_SCALE * (jax.nn.sigmoid(logits) - target.T.astype(jnp.float32))
    output_grad = jnp.dot(
        logit_grad, head_weight.astype(jnp.float32).T, precision=lax.Precision.HIGHEST
    )
    grad_low = output_grad.astype(jnp.bfloat16)
    proj_term = jnp.dot(mixed.T, grad_low, preferred_element_type=jnp.float32)
    mixed_grad = jnp.dot(grad_low, proj_weight.T, preferred_element_type=jnp.float32).astype(
        jnp.bfloat16
    )
    mixed_grad = mixed_grad.reshape(token_count, head_count, HEAD)
    value_grad = jnp.einsum(
        "hqk,qhd->khd", attend_low, mixed_grad, preferred_element_type=jnp.float32
    )
    attend_grad = jnp.einsum("qhd,khd->hqk", mixed_grad, values, preferred_element_type=jnp.float32)
    score_grad = (
        attend * (attend_grad - jnp.sum(attend_grad * attend, axis=-1, keepdims=True)) * score_scale
    )
    score_low = score_grad.astype(jnp.bfloat16)
    query_grad = jnp.einsum("hqk,khd->qhd", score_low, key_rows, preferred_element_type=jnp.float32)
    key_grad = jnp.einsum("hqk,qhd->khd", score_low, queries, preferred_element_type=jnp.float32)
    qkv_grad = jnp.concatenate(
        [
            query_grad.reshape(token_count, inner_width),
            key_grad.reshape(token_count, inner_width),
            value_grad.reshape(token_count, inner_width),
        ],
        axis=1,
    ).astype(jnp.bfloat16)
    qkv_term = jnp.dot(normed.T, qkv_grad, preferred_element_type=jnp.float32)
    normed_grad = jnp.dot(qkv_grad, qkv_weight.T, preferred_element_type=jnp.float32)
    grad_mean = jnp.mean(normed_grad, axis=-1, keepdims=True)
    grad_along = jnp.mean(normed_grad * unit_rows, axis=-1, keepdims=True)
    cell_grad = output_grad + inv_std * (normed_grad - grad_mean - unit_rows * grad_along)
    return (cell_grad.astype(jnp.bfloat16), qkv_term, proj_term)


def to_windows(grid):
    cells_x, cells_y, cells_z = (grid.shape[0], grid.shape[1], grid.shape[2])
    trailing = grid.shape[3:]
    shaped = grid.reshape(
        (cells_x // WIN, WIN, cells_y // WIN, WIN, cells_z // WIN, WIN) + trailing
    )
    order = (0, 2, 4, 1, 3, 5) + tuple(range(6, 6 + len(trailing)))
    return shaped.transpose(order).reshape((-1, WIN**3) + trailing)


def from_windows(windows, cells_x, cells_y, cells_z):
    width = windows.shape[-1]
    shaped = windows.reshape(cells_x // WIN, cells_y // WIN, cells_z // WIN, WIN, WIN, WIN, width)
    return shaped.transpose(0, 3, 1, 4, 2, 5, 6).reshape(cells_x, cells_y, cells_z, width)


def region_grid(cells_x, cells_y, cells_z):
    margin = WIN // 2
    whole_x = cells_x * lax.axis_size("gy")
    whole_y = cells_y * lax.axis_size("gx")
    coord_x = lax.axis_index("gy") * cells_x + jnp.arange(cells_x, dtype=jnp.int32)
    coord_y = lax.axis_index("gx") * cells_y + jnp.arange(cells_y, dtype=jnp.int32)
    coord_z = jnp.arange(cells_z, dtype=jnp.int32)
    flag_x = (coord_x >= whole_x - margin).astype(jnp.int32)
    flag_y = (coord_y >= whole_y - margin).astype(jnp.int32)
    flag_z = (coord_z >= cells_z - margin).astype(jnp.int32)
    return flag_x[:, None, None] * 4 + flag_y[None, :, None] * 2 + flag_z[None, None, :]


def slot_select(wanted, count):
    rank = jnp.cumsum(wanted.astype(jnp.int32)) - 1
    chosen = wanted[None, :] & (rank[None, :] == jnp.arange(count, dtype=jnp.int32)[:, None])
    return chosen.astype(jnp.bfloat16)


def per_device(volume, affinity, window_dest, qkv_weight, proj_weight, head_weight):
    margin = WIN // 2
    cells_x, cells_y, cells_z, width = (
        volume.shape[1],
        volume.shape[2],
        volume.shape[3],
        volume.shape[4],
    )
    cells = WIN**3
    rim_first, rim_first_aff = passed_along((volume[:, :margin], affinity[:, :, :margin]), "gy", -1)
    grown = jnp.concatenate([volume[:, margin:], rim_first], axis=1)
    grown_aff = jnp.concatenate([affinity[:, :, margin:], rim_first_aff], axis=2)
    rim_second, rim_second_aff = passed_along(
        (grown[:, :, :margin], grown_aff[:, :, :, :margin]), "gx", -1
    )
    grown = jnp.concatenate([grown[:, :, margin:], rim_second], axis=2)
    grown_aff = jnp.concatenate([grown_aff[:, :, :, margin:], rim_second_aff], axis=3)
    grown = jnp.roll(grown[0], -margin, axis=2)
    grown_aff = jnp.roll(grown_aff[0], -margin, axis=3)
    tokens = to_windows(grown)
    targets = jnp.moveaxis(to_windows(jnp.moveaxis(grown_aff, 0, -1)), -1, 1)
    regions = to_windows(region_grid(cells_x, cells_y, cells_z))
    destinations = window_dest.reshape(-1)
    window_count = destinations.shape[0]
    group_size = lax.axis_size("ga")
    balance_count = window_count // 2
    zero_qkv = jnp.zeros(qkv_weight.shape, jnp.float32)
    zero_proj = jnp.zeros(proj_weight.shape, jnp.float32)

    def step(carry, item):
        cell_grad, qkv_term, proj_term = window_grads(
            item[0], item[1], item[2], qkv_weight, proj_weight, head_weight
        )
        return ((carry[0] + qkv_term, carry[1] + proj_term), cell_grad)

    slots = window_count // 4
    reach = min(HOPS, group_size - 1)
    own = lax.axis_index("ga")
    relative = jnp.where(destinations < group_size, (destinations - own) % group_size, -1)
    region_low = (regions + 1).astype(jnp.bfloat16)

    def pack(select_low):
        packed_tokens = jnp.einsum(
            "sw,wtd->std", select_low, tokens, preferred_element_type=jnp.float32
        ).astype(jnp.bfloat16)
        packed_targets = jnp.einsum(
            "sw,wat->sat", select_low, targets, preferred_element_type=jnp.float32
        ).astype(jnp.bfloat16)
        packed_regions = (
            jnp.einsum("sw,wt->st", select_low, region_low, preferred_element_type=jnp.float32)
            - 1.0
        ).astype(jnp.bfloat16)
        return (packed_tokens, packed_targets, packed_regions)

    kept_select = slot_select(relative == 0, balance_count)
    gathered = [pack(kept_select)]
    selects = []
    for offset in range(1, reach + 1):
        moved_select = slot_select(relative == offset, slots)
        selects.append(moved_select)
        gathered.append(passed_along(for_sending(pack(moved_select)), "ga", offset))
    got_tokens = jnp.concatenate([item[0] for item in gathered], axis=0)
    got_targets = jnp.concatenate([item[1] for item in gathered], axis=0)
    got_regions = jnp.concatenate([item[2] for item in gathered], axis=0)
    filled = got_regions[:, 0].astype(jnp.float32) >= 0.0
    filled_rank = jnp.cumsum(filled.astype(jnp.int32)) - 1
    pick = filled[None, :] & (
        filled_rank[None, :] == jnp.arange(balance_count, dtype=jnp.int32)[:, None]
    )
    pick_low = pick.astype(jnp.bfloat16)
    work_tokens = jnp.einsum(
        "bs,std->btd", pick_low, got_tokens, preferred_element_type=jnp.float32
    ).astype(jnp.bfloat16)
    work_targets = jnp.einsum(
        "bs,sat->bat", pick_low, got_targets, preferred_element_type=jnp.float32
    ).astype(jnp.bfloat16)
    work_regions = jnp.einsum(
        "bs,st->bt", pick_low, got_regions, preferred_element_type=jnp.float32
    ).astype(jnp.int32)
    (total_qkv, total_proj), work_grads = lax.scan(
        step, (zero_qkv, zero_proj), (work_tokens, work_targets, work_regions)
    )
    send_back = jnp.einsum(
        "bs,btd->std", pick_low, work_grads, preferred_element_type=jnp.float32
    ).astype(jnp.bfloat16)
    gathered_grad = jnp.einsum(
        "sw,std->wtd", kept_select, send_back[:balance_count], preferred_element_type=jnp.float32
    )
    for offset in range(1, reach + 1):
        begin = balance_count + (offset - 1) * slots
        returned = passed_along(send_back[begin : begin + slots], "ga", -offset)
        gathered_grad = gathered_grad + jnp.einsum(
            "sw,std->wtd", selects[offset - 1], returned, preferred_element_type=jnp.float32
        )
    window_grad = gathered_grad.astype(jnp.bfloat16)
    grid_grad = from_windows(window_grad, cells_x, cells_y, cells_z)
    grid_grad = jnp.roll(grid_grad, margin, axis=2)
    back_second = passed_along(grid_grad[:, cells_y - margin :], "gx", 1)
    grid_grad = jnp.concatenate([back_second, grid_grad[:, : cells_y - margin]], axis=1)
    back_first = passed_along(grid_grad[cells_x - margin :], "gy", 1)
    grid_grad = jnp.concatenate([back_first, grid_grad[: cells_x - margin]], axis=0)
    share_qkv, share_proj = (
        lax.psum_scatter(total_qkv, "ga", scatter_dimension=0, tiled=True),
        lax.psum_scatter(total_proj, "ga", scatter_dimension=1, tiled=True),
    )
    summed_qkv, summed_proj = lax.psum((share_qkv, share_proj), ("gy", "gx"))
    live_cells = lax.axis_size("gy") * lax.axis_size("gx") * group_size * balance_count * cells
    factor = float(live_cells) ** (-0.5)
    return (grid_grad[None], summed_qkv * factor, summed_proj * factor)


def solution(mesh):
    placed = (
        P("ga", "gy", "gx", None, None),
        P("ga", None, "gy", "gx", None),
        P("ga", "gy", "gx", None),
        P(),
        P(),
        P(),
    )
    return jax.shard_map(
        per_device,
        mesh=mesh,
        in_specs=placed,
        out_specs=(P("ga", "gy", "gx", None, None), P("ga", None), P(None, "ga")),
        check_vma=False,
    )
```

profile of v0, /device:TPU:2, one launch (start us, length us, event | category | flops | bytes accessed | tf_op | source)
XLA Modules:
  0.0 543.4 jit_solution(7793813690417377618)
XLA Ops:
  8.9 1.2 bitcast_convert_fusion.7
  11.0 2.0 collective-permute-start.1
  13.0 1.9 slice.83
  16.1 2.8 collective-permute-start.6
  19.9 1.7 slice.82
  22.0 8.0 %collective-permute-done.6 = bf16[1,3,3,14,7]{3,4,2,1,0:T(8,128)(2,1)S(1)} collective-permute-done((bf16[1,3,3,14,7]{3,4,2,1,0:T(8,128)(2,1)S(1)}, bf16[1,3,3,14,7]{3,4,2,1,0:T(8,128)(2,1)S(1)}, u32[]{:S(2)}, u32[]{:S(2)}) %collective-permute-start.6) | collective-permute-done | bytes 1796 | tf_op jit(solution)/shard_map/ppermute | solution.py:18
  30.1 4.6 collective-permute-start.7
  34.8 4.4 collective-permute-done.7
  40.6 1.0 pad_maximum_fusion.12
  41.6 4.6 collective-permute-start.3
  47.5 1.4 fusion.73
  48.9 17.7 %collective-permute-done.3 = bf16[1,14,3,7,768]{4,3,2,1,0:T(8,128)(2,1)S(1)} collective-permute-done((bf16[1,14,3,7,768]{4,3,2,1,0:T(8,128)(2,1)S(1)}, bf16[1,14,3,7,768]{4,3,2,1,0:T(8,128)(2,1)S(1)}, u32[]{:S(2)}, u32[]{:S(2)}) %collective-permute-start.3) | collective-permute-done | bytes 451616 | tf_op jit(solution)/shard_map/ppermute | solution.py:18
  68.0 1.2 pad_maximum_fusion.5
  69.3 1.7 copy.101
  71.0 2.1 reshape.477
  73.1 3.0 fusion.113
  76.1 1.2 fusion.111
  77.6 1.6 collective-permute-start.5
  79.3 1.2 convolution_convert_fusion.3
  80.6 12.6 %collective-permute-done.4 = bf16[1,343,768]{2,1,0:T(8,128)(2,1)S(1)} collective-permute-done((bf16[1,343,768]{2,1,0:T(8,128)(2,1)S(1)}, bf16[1,343,768]{2,1,0:T(8,128)(2,1)S(1)}, u32[]{:S(2)}, u32[]{:S(2)}) %collective-permute-start.4) | collective-permute-done | bytes 526880 | tf_op jit(solution)/shard_map/ppermute | solution.py:18
  95.5 3.7 fusion.74
  99.9 119.2 %while.15 = (s32[]{:T(128)}, f32[768,1152]{1,0:T(8,128)}, f32[384,768]{1,0:T(8,128)S(1)}, bf16[2,343,768]{2,1,0:T(8,128)(2,1)}, bf16[2,343,768]{2,1,0:T(8,128)(2...) while((s32[]{:T(128)}, f32[768,1152]{1,0:T(8,128)}, ...), condition=%wide.region_12.13_spmd.clone, body=%wide.region_4.12_spmd.clone.sunk | while | flops 3029209600 | bytes 97110760 | solution.py:209
  100.6 2.4 convolution_convert_fusion.9
  103.3 0.9 copy.112
  104.4 6.1 %fusion.227 = (f32[12,343]{1,0:T(8,128)S(1)}, f32[12,343,343]{1,2,0:T(8,128)}) fusion(pred[343,343]{0,1:T(8,128)(4,1)S(1)} %broadcast_compare_fusion.4, bf16[343,12,32]{0,2,1:T(8,128)(2,1)S(1)} %bitcast.327, bf16[343,12,32]{0,2,1:T(8,128)(2,1)} %bitcast.329), kind=kOutput, calls=%fused_computation.202.clone.1 | convolution fusion | flops 96001928 | bytes 6308113 | tf_op jit(solution)/shard_map/while/body/eval_jaxpr/sub | solution.py:48
  110.8 3.6 fusion.228
  116.4 2.3 convolution_convert_fusion.10
  118.7 1.8 copy.113
  120.5 5.0 fusion.232
  125.5 10.9 %fusion.234 = bf16[12,32,343]{2,1,0:T(8,128)(2,1)} fusion(bf16[343,12,32]{0,2,1:T(8,128)(2,1)} %bitcast.330, f32[12,343,343]{1,2,0:T(8,128)} %fusion.232, f32[12,343,343]{1,2,0:T(8,128)} %get-tuple-element.243, f32[12,343]{1,0:T(8,128)S(1)} %get-tuple-element.244), kind=kOutput, calls=%fused_computation.32.clone.1 | convolution fusion | flops 100373120 | bytes 11837616 | tf_op jit(solution)/shard_map/while/body/eval_jaxpr/hqk,khd->qhd/dot_general | solution.py:77
  136.5 11.0 %fusion.233 = bf16[12,32,343]{2,1,0:T(8,128)(2,1)} fusion(bf16[343,12,32]{0,2,1:T(8,128)(2,1)} %bitcast.328, f32[12,343,343]{1,2,0:T(8,128)} %fusion.232, f32[12,343,343]{1,2,0:T(8,128)} %get-tuple-element.243, f32[12,343]{1,0:T(8,128)S(1)} %get-tuple-element.244), kind=kOutput, calls=%fused_computation.33.clone.1 | convolution fusion | flops 100373120 | bytes 11837616 | tf_op jit(solution)/shard_map/while/body/eval_jaxpr/hqk,qhd->khd/dot_general | solution.py:78
  147.4 4.0 fusion.231
  151.5 1.1 fusion.235
  152.7 1.2 fusion.236
  153.9 4.3 convolution_add_fusion.6
  159.4 2.4 convolution_convert_fusion.9
  163.3 6.1 %fusion.227 = (f32[12,343]{1,0:T(8,128)S(1)}, f32[12,343,343]{1,2,0:T(8,128)}) fusion(pred[343,343]{0,1:T(8,128)(4,1)S(1)} %broadcast_compare_fusion.4, bf16[343,12,32]{0,2,1:T(8,128)(2,1)S(1)} %bitcast.327, bf16[343,12,32]{0,2,1:T(8,128)(2,1)} %bitcast.329), kind=kOutput, calls=%fused_computation.202.clone.1 | convolution fusion | flops 96001928 | bytes 6308113 | tf_op jit(solution)/shard_map/while/body/eval_jaxpr/sub | solution.py:48
  169.7 3.6 fusion.228
  175.3 2.3 convolution_convert_fusion.10
  177.6 1.8 copy.113
  179.4 5.0 fusion.232
  184.4 10.9 %fusion.234 = bf16[12,32,343]{2,1,0:T(8,128)(2,1)} fusion(bf16[343,12,32]{0,2,1:T(8,128)(2,1)} %bitcast.330, f32[12,343,343]{1,2,0:T(8,128)} %fusion.232, f32[12,343,343]{1,2,0:T(8,128)} %get-tuple-element.243, f32[12,343]{1,0:T(8,128)S(1)} %get-tuple-element.244), kind=kOutput, calls=%fused_computation.32.clone.1 | convolution fusion | flops 100373120 | bytes 11837616 | tf_op jit(solution)/shard_map/while/body/eval_jaxpr/hqk,khd->qhd/dot_general | solution.py:77
  195.4 11.0 %fusion.233 = bf16[12,32,343]{2,1,0:T(8,128)(2,1)} fusion(bf16[343,12,32]{0,2,1:T(8,128)(2,1)} %bitcast.328, f32[12,343,343]{1,2,0:T(8,128)} %fusion.232, f32[12,343,343]{1,2,0:T(8,128)} %get-tuple-element.243, f32[12,343]{1,0:T(8,128)S(1)} %get-tuple-element.244), kind=kOutput, calls=%fused_computation.33.clone.1 | convolution fusion | flops 100373120 | bytes 11837616 | tf_op jit(solution)/shard_map/while/body/eval_jaxpr/hqk,qhd->khd/dot_general | solution.py:78
  206.3 4.0 fusion.231
  210.4 1.1 fusion.235
  211.6 1.2 fusion.236
  212.8 5.4 %convolution_add_fusion.6 = f32[768,1152]{1,0:T(8,128)} fusion(f32[768,1152]{1,0:T(8,128)} %get-tuple-element.263, pred[]{:T(512)S(6)} %compare.25, bf16[343,384]{0,1:T(8,128)(2,1)} %bitcast.326, bf16[343,384]{0,1:T(8,128)(2,1)} %bitcast.323, bf16[343,384]{0,1:T(8,128)(2,1)} %bitcast.321, f32[343]{0:T(512)S(1)} %add_rsqrt_fusion.2, ...), kind=kOutput, calls=%fused_computation.8.clone.1 | convolution fusion | flops 612122880 | bytes 8400645 | tf_op jit(solution)/shard_map/while/body/eval_jaxpr/dot_general | solution.py:87
  219.2 1.4 copy.77
  221.5 2.8 convolution_convert_fusion.2
  224.3 2.0 fusion.133
  226.6 5.7 %collective-permute-start.10 = (bf16[1,343,768]{2,1,0:T(8,128)(2,1)S(1)}, bf16[1,343,768]{2,1,0:T(8,128)(2,1)S(1)}, u32[]{:S(2)}, u32[]{:S(2)}) collective-permute-start(bf16[1,343,768]{2,1,0:T(8,128)(2,1)S(1)} %copy.74), channel_id=1, source_target_pairs={{1,0},{2,1},{3,2},{4,3},{5,4},{6,5},{7,6},{8,7},{9,8},{10,9},{11,1... | collective-permute-start | bytes 1580552 | tf_op jit(solution)/shard_map/ppermute | solution.py:18
  232.3 5.2 collective-permute-done.11
  237.6 9.8 %collective-permute-done.10 = bf16[1,343,768]{2,1,0:T(8,128)(2,1)S(1)} collective-permute-done((bf16[1,343,768]{2,1,0:T(8,128)(2,1)S(1)}, bf16[1,343,768]{2,1,0:T(8,128)(2,1)S(1)}, u32[]{:S(2)}, u32[]{:S(2)}) %collective-permute-start.10) | collective-permute-done | bytes 526880 | tf_op jit(solution)/shard_map/ppermute | solution.py:18
  247.4 4.5 add_convert_fusion
  252.0 4.4 reshape.482
  257.9 2.2 collective-permute-start.12
  260.1 26.7 %collective-permute-done.12 = bf16[14,3,7,768]{3,2,1,0:T(8,128)(2,1)S(1)} collective-permute-done((bf16[14,3,7,768]{3,2,1,0:T(8,128)(2,1)S(1)}, bf16[14,3,7,768]{3,2,1,0:T(8,128)(2,1)S(1)}, u32[]{:S(2)}, u32[]{:S(2)}) %collective-permute-start.12) | collective-permute-done | bytes 451616 | tf_op jit(solution)/shard_map/ppermute | solution.py:18
  287.0 1.6 collective-permute-start.13
  288.6 11.0 %reduce-scatter.5.cloned.1.call-done = f32[384,48]{0,1:T(8,128)} async-done(((f32[384,768]{0,1:T(8,128)}), f32[384,48]{0,1:T(8,128)}) %reduce-scatter.5.cloned.1.call-update) | async-done | bytes 73744 | tf_op jit(solution)/shard_map/reduce_scatter | solution.py:233
  299.6 72.3 %reduce-scatter.3.cloned.1.call-done = f32[48,1152]{1,0:T(8,128)} async-done(((f32[768,1152]{1,0:T(8,128)}), f32[48,1152]{1,0:T(8,128)}) %reduce-scatter.3.cloned.1.call-update) | async-done | bytes 221200 | tf_op jit(solution)/shard_map/reduce_scatter | solution.py:232
  371.9 3.4 fusion.71
  375.3 158.2 %all-reduce.3.cloned.1.call-done = (f32[48,1152]{1,0:T(8,128)}, f32[384,48]{0,1:T(8,128)}) async-done(((f32[48,1152]{1,0:T(8,128)}, f32[384,48]{0,1:T(8,128)}), (f32[48,1152]{1,0:T(8,128)}, f32[384,48]{0,1:T(8,128)})) %all-reduce.3.cloned.1.call-update) | async-done | bytes 294928 | tf_op jit(solution)/shard_map/psum | solution.py:235
  533.5 1.6 broadcast_multiply_fusion.3
  535.1 1.5 broadcast_multiply_fusion.4
  (181 shorter events, 24.7 us)
Async XLA Ops:
  7.2 292.4 %reduce-scatter.5.cloned.1.call-start = ((), (), s32[]{:S(2)}) async-start(), calls=%async_computation.3 | async-start | bytes 1253376 | tf_op jit(solution)/shard_map/reduce_scatter | solution.py:233
  10.1 66.0 %copy-start.13 = (s32[1,1,1,4]{3,2,1,0:T(1,128)}, s32[1,1,1,4]{3,2,1,0:T(1,128)S(1)}, u32[]{:S(2)}) copy-start(s32[1,1,1,4]{3,2,1,0:T(1,128)S(1)} %get-tuple-element.148) | copy-start | bytes 52
  10.6 11.0 %collective-permute-start = (bf16[1,343]{1,0:T(2,128)(2,1)S(1)}, bf16[1,343]{1,0:T(2,128)(2,1)S(1)}, u32[]{:S(2)}, u32[]{:S(2)}) collective-permute-start(bf16[1,343]{1,0:T(2,128)(2,1)S(1)} %convert_element_type.190), channel_id=1, source_target_pairs={{15,0},{0,1},{1,2},{2,3},{3,4},{4,5},{5,6},{6,7},{7,8},{8,9},{9,10... | collective-permute-start | bytes 2066 | tf_op jit(solution)/shard_map/ppermute | solution.py:18
  10.9 65.2 %copy-start.15 = (pred[4]{0:T(512)(128)(4,1)}, pred[4]{0:T(512)(128)(4,1)S(1)}, u32[]{:S(2)}) copy-start(pred[4]{0:T(512)(128)(4,1)S(1)} %fusion.100) | copy-start | bytes 16
  11.0 10.6 %collective-permute-start.1 = (bf16[1,343]{1,0:T(2,128)(2,1)S(1)}, bf16[1,343]{1,0:T(2,128)(2,1)S(1)}, u32[]{:S(2)}, u32[]{:S(2)}) collective-permute-start(bf16[1,343]{1,0:T(2,128)(2,1)S(1)} %convert_element_type.193), channel_id=1, source_target_pairs={{14,0},{15,1},{0,2},{1,3},{2,4},{3,5},{4,6},{5,7},{6,8},{7,9},{8,1... | collective-permute-start | bytes 2066 | tf_op jit(solution)/shard_map/ppermute | solution.py:18
  14.9 25.8 %collective-permute-start.2 = (bf16[1,3,14,7,768]{4,3,2,1,0:T(8,128)(2,1)}, bf16[1,3,14,7,768]{4,3,2,1,0:T(8,128)(2,1)}, u32[]{:S(2)}, u32[]{:S(2)}) collective-permute-start(bf16[1,3,14,7,768]{4,3,2,1,0:T(8,128)(2,1)} %slice.83), channel_id=1, source_target_pairs={{64,0},{128,64},{192,128},{0,192},{65,1},{129,65},{193,129},{1,193... | collective-permute-start | bytes 1354760 | tf_op jit(solution)/shard_map/ppermute | solution.py:18
  16.1 13.9 %collective-permute-start.6 = (bf16[1,3,3,14,7]{3,4,2,1,0:T(8,128)(2,1)S(1)}, bf16[1,3,3,14,7]{3,4,2,1,0:T(8,128)(2,1)S(1)}, u32[]{:S(2)}, u32[]{:S(2)}) collective-permute-start(bf16[1,3,3,14,7]{3,4,2,1,0:T(8,128)(2,1)S(1)} %slice.89), channel_id=1, source_target_pairs={{64,0},{128,64},{192,128},{0,192},{65,1},{129,65},{193,129},{1,193... | collective-permute-start | bytes 5300 | tf_op jit(solution)/shard_map/ppermute | solution.py:18
  19.7 59.6 %copy-start.18 = (pred[2,4]{1,0:T(4,128)(4,1)}, pred[2,4]{1,0:T(4,128)(4,1)S(1)}, u32[]{:S(2)}) copy-start(pred[2,4]{1,0:T(4,128)(4,1)S(1)} %compare_and_fusion.1) | copy-start | bytes 28
  19.9 1.7 copy-start.11
  21.9 73.6 %copy-start.20 = (pred[2,4]{1,0:T(4,128)(4,1)}, pred[2,4]{1,0:T(4,128)(4,1)S(1)}, u32[]{:S(2)}) copy-start(pred[2,4]{1,0:T(4,128)(4,1)S(1)} %compare_and_fusion) | copy-start | bytes 28
  30.1 9.2 %collective-permute-start.7 = (bf16[1,3,14,3,7]{3,4,2,1,0:T(8,128)(2,1)S(1)}, bf16[1,3,14,3,7]{3,4,2,1,0:T(8,128)(2,1)S(1)}, u32[]{:S(2)}, u32[]{:S(2)}) collective-permute-start(bf16[1,3,14,3,7]{3,4,2,1,0:T(8,128)(2,1)S(1)} %pad_maximum_fusion.13), channel_id=1, source_target_pairs={{16,0},{32,16},{48,32},{0,48},{17,1},{33,17},{49,33},{1,49},{18,2}... | collective-permute-start | bytes 5300 | tf_op jit(solution)/shard_map/ppermute | solution.py:18
  41.6 24.9 %collective-permute-start.3 = (bf16[1,14,3,7,768]{4,3,2,1,0:T(8,128)(2,1)S(1)}, bf16[1,14,3,7,768]{4,3,2,1,0:T(8,128)(2,1)S(1)}, u32[]{:S(2)}, u32[]{:S(2)}) collective-permute-start(bf16[1,14,3,7,768]{4,3,2,1,0:T(8,128)(2,1)S(1)} %pad_maximum_fusion.12), channel_id=1, source_target_pairs={{16,0},{32,16},{48,32},{0,48},{17,1},{33,17},{49,33},{1,49},{18,2}... | collective-permute-start | bytes 1354760 | tf_op jit(solution)/shard_map/ppermute | solution.py:18
  46.4 32.8 %collective-permute-start.8 = (bf16[1,3,343]{2,0,1:T(2,128)(2,1)S(1)}, bf16[1,3,343]{2,0,1:T(2,128)(2,1)S(1)}, u32[]{:S(2)}, u32[]{:S(2)}) collective-permute-start(bf16[1,3,343]{2,0,1:T(2,128)(2,1)S(1)} %copy.69), channel_id=1, source_target_pairs={{15,0},{0,1},{1,2},{2,3},{3,4},{4,5},{5,6},{6,7},{7,8},{8,9},{9,10... | collective-permute-start | bytes 6182 | tf_op jit(solution)/shard_map/ppermute | solution.py:18
  46.5 32.6 %collective-permute-start.9 = (bf16[1,3,343]{2,0,1:T(2,128)(2,1)S(1)}, bf16[1,3,343]{2,0,1:T(2,128)(2,1)S(1)}, u32[]{:S(2)}, u32[]{:S(2)}) collective-permute-start(bf16[1,3,343]{2,0,1:T(2,128)(2,1)S(1)} %copy.70), channel_id=1, source_target_pairs={{14,0},{15,1},{0,2},{1,3},{2,4},{3,5},{4,6},{5,7},{6,8},{7,9},{8,1... | collective-permute-start | bytes 6182 | tf_op jit(solution)/shard_map/ppermute | solution.py:18
  73.1 3.0 copy-start.9
  77.4 15.8 %collective-permute-start.4 = (bf16[1,343,768]{2,1,0:T(8,128)(2,1)S(1)}, bf16[1,343,768]{2,1,0:T(8,128)(2,1)S(1)}, u32[]{:S(2)}, u32[]{:S(2)}) collective-permute-start(bf16[1,343,768]{2,1,0:T(8,128)(2,1)S(1)} %copy.102), channel_id=1, source_target_pairs={{15,0},{0,1},{1,2},{2,3},{3,4},{4,5},{5,6},{6,7},{7,8},{8,9},{9,10... | collective-permute-start | bytes 1580552 | tf_op jit(solution)/shard_map/ppermute | solution.py:18
  77.6 17.1 %collective-permute-start.5 = (bf16[1,343,768]{2,1,0:T(8,128)(2,1)S(1)}, bf16[1,343,768]{2,1,0:T(8,128)(2,1)S(1)}, u32[]{:S(2)}, u32[]{:S(2)}) collective-permute-start(bf16[1,343,768]{2,1,0:T(8,128)(2,1)S(1)} %copy.103), channel_id=1, source_target_pairs={{14,0},{15,1},{0,2},{1,3},{2,4},{3,5},{4,6},{5,7},{6,8},{7,9},{8,1... | collective-permute-start | bytes 1580552 | tf_op jit(solution)/shard_map/ppermute | solution.py:18
  99.2 0.7 copy-start.10
  103.3 7.2 %copy-start.6 = (bf16[343,384]{0,1:T(8,128)(2,1)}, bf16[343,384]{0,1:T(8,128)(2,1)S(1)}, u32[]{:S(2)}) copy-start(bf16[343,384]{0,1:T(8,128)(2,1)S(1)} %copy.111) | copy-start | bytes 790276 | tf_op jit(solution)/shard_map/while
  110.7 3.6 copy-start
  110.8 4.3 copy-start.2
  114.4 0.7 copy-start.7
  147.4 4.1 copy-start.3
  147.4 4.1 copy-start.4
  147.4 4.1 copy-start.17
  151.5 1.2 copy-start.5
  153.9 4.3 copy-start.8
  162.2 7.2 %copy-start.6 = (bf16[343,384]{0,1:T(8,128)(2,1)}, bf16[343,384]{0,1:T(8,128)(2,1)S(1)}, u32[]{:S(2)}) copy-start(bf16[343,384]{0,1:T(8,128)(2,1)S(1)} %copy.111) | copy-start | bytes 790276 | tf_op jit(solution)/shard_map/while
  169.6 3.6 copy-start
  169.6 4.3 copy-start.2
  173.3 0.7 copy-start.7
  206.3 4.1 copy-start.3
  206.3 4.1 copy-start.4
  206.3 4.1 copy-start.17
  210.4 1.2 copy-start.5
  212.8 5.4 %copy-start.8 = (bf16[12,32,343]{2,1,0:T(8,128)(2,1)S(1)}, bf16[12,32,343]{2,1,0:T(8,128)(2,1)}, u32[]{:S(2)}) copy-start(bf16[12,32,343]{2,1,0:T(8,128)(2,1)} %copy-done.7) | copy-start | bytes 790276 | tf_op jit(solution)/shard_map/while
  220.6 0.8 copy-start.21
  220.6 151.2 %reduce-scatter.3.cloned.1.call-start = ((), (), s32[]{:S(2)}) async-start(), calls=%async_computation.2 | async-start | bytes 3760128 | tf_op jit(solution)/shard_map/reduce_scatter | solution.py:232
  221.4 312.1 %all-reduce.3.cloned.1.call-start = ((), (), s32[]{:S(2)}) async-start(), calls=%async_computation.4 | async-start | bytes 589824 | tf_op jit(solution)/shard_map/psum | solution.py:235
  226.2 6.1 %copy-start.14 = (s32[1,1,1,4]{3,2,1,0:T(1,128)S(1)}, s32[1,1,1,4]{3,2,1,0:T(1,128)}, u32[]{:S(2)}) copy-start(s32[1,1,1,4]{3,2,1,0:T(1,128)} %copy-done.13) | copy-start | bytes 52
  226.3 6.1 %copy-start.16 = (pred[4]{0:T(512)(128)(4,1)S(1)}, pred[4]{0:T(512)(128)(4,1)}, u32[]{:S(2)}) copy-start(pred[4]{0:T(512)(128)(4,1)} %copy-done.15) | copy-start | bytes 16
  226.3 11.2 %collective-permute-start.11 = (bf16[1,343,768]{2,1,0:T(8,128)(2,1)S(1)}, bf16[1,343,768]{2,1,0:T(8,128)(2,1)S(1)}, u32[]{:S(2)}, u32[]{:S(2)}) collective-permute-start(bf16[1,343,768]{2,1,0:T(8,128)(2,1)S(1)} %copy.75), channel_id=1, source_target_pairs={{2,0},{3,1},{4,2},{5,3},{6,4},{7,5},{8,6},{9,7},{10,8},{11,9},{12,... | collective-permute-start | bytes 1580552 | tf_op jit(solution)/shard_map/ppermute | solution.py:18
  226.6 20.8 %copy-start.12 = (f32[4]{0:T(128)S(1)}, f32[4]{0:T(128)}, u32[]{:S(2)}) copy-start(f32[4]{0:T(128)} %get-tuple-element.147) | copy-start | bytes 52
  226.6 20.8 %copy-start.19 = (pred[2,4]{1,0:T(4,128)(4,1)S(1)}, pred[2,4]{1,0:T(4,128)(4,1)}, u32[]{:S(2)}) copy-start(pred[2,4]{1,0:T(4,128)(4,1)} %copy-done.18) | copy-start | bytes 28
  226.6 20.7 %collective-permute-start.10 = (bf16[1,343,768]{2,1,0:T(8,128)(2,1)S(1)}, bf16[1,343,768]{2,1,0:T(8,128)(2,1)S(1)}, u32[]{:S(2)}, u32[]{:S(2)}) collective-permute-start(bf16[1,343,768]{2,1,0:T(8,128)(2,1)S(1)} %copy.74), channel_id=1, source_target_pairs={{1,0},{2,1},{3,2},{4,3},{5,4},{6,5},{7,6},{8,7},{9,8},{10,9},{11,1... | collective-permute-start | bytes 1580552 | tf_op jit(solution)/shard_map/ppermute | solution.py:18
  257.7 29.4 %copy-start.1 = (bf16[14,14,4,768]{3,2,1,0:T(4,128)(2,1)}, bf16[14,14,4,768]{3,2,1,0:T(4,128)(2,1)S(1)}, u32[]{:S(2)}) copy-start(bf16[14,14,4,768]{3,2,1,0:T(4,128)(2,1)S(1)} %slice.121) | copy-start | bytes 3612676
  257.9 28.9 %collective-permute-start.12 = (bf16[14,3,7,768]{3,2,1,0:T(8,128)(2,1)S(1)}, bf16[14,3,7,768]{3,2,1,0:T(8,128)(2,1)S(1)}, u32[]{:S(2)}, u32[]{:S(2)}) collective-permute-start(bf16[14,3,7,768]{3,2,1,0:T(8,128)(2,1)S(1)} %pad_maximum_fusion.11), channel_id=1, source_target_pairs={{48,0},{0,16},{16,32},{32,48},{49,1},{1,17},{17,33},{33,49},{50,2}... | collective-permute-start | bytes 1354760 | tf_op jit(solution)/shard_map/ppermute | solution.py:18
  287.0 84.9 %collective-permute-start.13 = (bf16[3,14,7,768]{3,2,1,0:T(8,128)(2,1)S(1)}, bf16[3,14,7,768]{3,2,1,0:T(8,128)(2,1)S(1)}, u32[]{:S(2)}, u32[]{:S(2)}) collective-permute-start(bf16[3,14,7,768]{3,2,1,0:T(8,128)(2,1)S(1)} %pad_maximum_fusion.10), channel_id=1, source_target_pairs={{192,0},{0,64},{64,128},{128,192},{193,1},{1,65},{65,129},{129,193... | collective-permute-start | bytes 1354760 | tf_op jit(solution)/shard_map/ppermute | solution.py:18
Sparse Core Ops, SparseCore 0:
  220.8 78.7 reduce-scatter.4
  302.1 69.6 reduce-scatter.2
  374.6 158.8 all-reduce.2
where the time goes:
time: 550 us; the launch traced here: 543 us
  waiting for transfers between devices  327 us (59%)
  matrix products  124 us (23%)
  local copies, waits for them, and re-layouts  30.1 us (5%)
  starting transfers between devices  27 us (5%)
  other arithmetic  19.4 us (4%)
  between operations  14.5 us (3%)
    psum x1, waiting for transfers between devices, per_device(): summed_qkv, summed_proj = lax.psum((share_qkv, share_proj), ('gy', 'gx'))  158 us
    ppermute x14, waiting for transfers between devices, passed_along(): return lax.ppermute(block, axis, route)  85 us
    reduce_scatter x1, waiting for transfers between devices, per_device(): lax.psum_scatter(total_qkv, 'ga', scatter_dimension=0, tiled=True)  72.3 us
    ppermute x14, starting transfers between devices, passed_along(): return lax.ppermute(block, axis, route)  26.9 us
    dot_general x2, matrix products, window_grads(): jnp.einsum('hqk,qhd->khd', score_low, queries, preferred_element_type=jnp...  21.9 us
    dot_general x2, matrix products, window_grads(): jnp.einsum('hqk,khd->qhd', score_low, key_rows, preferred_element_type=jn...  21.8 us
    sub x2, matrix products, window_grads(): exponent = jnp.exp(scores - row_max)  12.3 us
  transfers between devices with their start and end apart: 17, of which 11 were waited for; matrix products, arithmetic and copies ran while one was open for 8% of the time, Pallas kernels for 0%

commit v1 on v0

v1 whole, which is shorter than its diff:
```python
import functools

import jax
import jax.numpy as jnp
import numpy as np
from jax import lax
from jax.experimental import pallas as pl
from jax.experimental.pallas import tpu as pltpu
from jax.sharding import PartitionSpec as P


HEAD = 32
WIN = 7
MARGIN = 3
LOSS_SCALE = 32.0
EPSILON = 1e-05
LOW_CELLS = 147
HIGH_CELLS = 196
LOW_ROWS = 160
HIGH_ROWS = 208
ROWS = LOW_ROWS + HIGH_ROWS
BLOCKS = ((0, LOW_ROWS, LOW_CELLS), (LOW_ROWS, HIGH_ROWS, HIGH_CELLS))
GROUP = 128
PER_GROUP = GROUP // HEAD
MASKED = -1e30
RIM_ROWS = 240
CORNER_ROWS = 64
LOW_Z = 3
OUTER = 4
F32 = jnp.float32
BF16 = jnp.bfloat16


def mm(a, b):
    return lax.dot_general(a, b, (((1,), (0,)), ((), ())), preferred_element_type=F32)


def mm_nt(a, b):
    return lax.dot_general(a, b, (((1,), (1,)), ((), ())), preferred_element_type=F32)


def row_cells():
    cells = np.full((ROWS, 3), -1)
    for z in range(WIN):
        for x in range(WIN):
            for y in range(WIN):
                if z < LOW_Z:
                    row = z * 49 + x * WIN + y
                else:
                    row = LOW_ROWS + (z - LOW_Z) * 49 + x * WIN + y
                cells[row] = (x, y, z)
    return cells


def source_rows():
    rest = 2 * WIN - MARGIN
    table = np.full((4, ROWS), -1)
    for row, (x, y, z) in enumerate(row_cells()):
        if x < 0:
            continue
        table[0, row] = (x * WIN + y) * 8 + z
        if y < OUTER:
            table[1, row] = (x * OUTER + y) * 8 + z
        else:
            table[1, row] = 224 + (x * MARGIN + y - OUTER) * WIN + z
        if x < OUTER:
            table[2, row] = (x * WIN + y) * 8 + z
        else:
            table[2, row] = 224 + ((x - OUTER) * rest + y) * WIN + z
        if x < OUTER and y < OUTER:
            table[3, row] = (x * OUTER + y) * 8 + z
        elif x < OUTER:
            table[3, row] = 128 + ((x + WIN) * MARGIN + y - OUTER) * WIN + z - 144
        elif y < OUTER:
            table[3, row] = 224 + ((x - OUTER) * rest + y + WIN) * WIN + z - 48
        else:
            table[3, row] = 416 + ((x - OUTER) * MARGIN + y - OUTER) * WIN + z
    table = np.pad(table, ((0, 0), (0, 3 * GROUP - ROWS)), constant_values=-1)
    return np.repeat(table[:, None, :], 8, axis=1).astype(np.float32)


def grid_rows():
    table = np.full((8, ROWS), -1)
    for row, (x, y, z) in enumerate(row_cells()):
        if x >= 0:
            table[:, row] = (x * WIN + y) * 8 + z
    return table.astype(np.int32)


def edge_code(index, edge_x, edge_y):
    by_row = jnp.floor((index + 0.5) * (1.0 / 7.0))
    y = index - 7.0 * by_row
    z = jnp.floor((by_row + 0.5) * (1.0 / 7.0))
    x = by_row - 7.0 * z
    on_x = jnp.where(x >= 4.0, edge_x, 0.0)
    on_y = jnp.where(y >= 4.0, edge_y, 0.0)
    return 2.0 * on_x + on_y


def head_masks():
    lane = lax.broadcasted_iota(jnp.int32, (1, GROUP), 1)
    return [
        jnp.where((lane >= h * HEAD) & (lane < (h + 1) * HEAD), 1.0, 0.0).astype(BF16)
        for h in range(PER_GROUP)
    ]


def take_own(vol_ref, aff_ref, own, xs, ys):
    count = len(xs) * len(ys)
    width = vol_ref.shape[-1]
    for i, x in enumerate(xs):
        at = slice(i * len(ys), (i + 1) * len(ys))
        own[at, 0:WIN, 0:width] = vol_ref[x, ys[0] : ys[-1] + 1].astype(F32)
        own[at, 0:WIN, width:] = aff_ref[x, ys[0] : ys[-1] + 1].astype(F32)
    rows = count * 8
    return own[0:count].reshape(rows, own.shape[-1]).astype(BF16)


def gather_rows(index, sources):
    depth = sources.shape[0]
    at = lax.broadcasted_iota(jnp.int32, (ROWS, depth), 1)
    column = index.T[:ROWS, 0:1].astype(jnp.int32)
    chosen = jnp.where(column == at, 1.0, 0.0).astype(BF16)
    return mm(chosen, sources)


def window_terms(info, window, cells, weights, outs, acc_q, acc_p, scratch):
    wqkv_ref, proj_ref, headt_ref = weights
    tok_ref, lg_ref, d_ref = outs
    qkv_s, mixed_s, mg_s, p_low, p_high, bias_low, bias_high = scratch
    inner, width = proj_ref.shape
    groups = inner // GROUP
    scale = HEAD ** (-0.5)
    p_refs = (p_low, p_high)
    bias_refs = (bias_low, bias_high)
    edge_x = jnp.where((info[4] != 0) & (window >= 2), 1.0, 0.0)
    edge_y = jnp.where((info[5] != 0) & (lax.rem(window, 2) == 1), 1.0, 0.0)
    for (_, rows, cells_here), bias in zip(BLOCKS, bias_refs):
        down = lax.broadcasted_iota(jnp.int32, (rows, 1), 0).astype(F32)
        along = lax.broadcasted_iota(jnp.int32, (1, rows), 1).astype(F32)
        same = edge_code(down, edge_x, edge_y) == edge_code(along, edge_x, edge_y)
        bias[...] = jnp.where(same & (along < cells_here), 0.0, MASKED)
    masks = head_masks()
    u = cells[:, :width]
    target = cells[:, width : width + 3]
    tok_ref[0] = u.astype(BF16)
    mean_row = jnp.mean(u, axis=-1, keepdims=True)
    centred = u - mean_row
    variance = jnp.mean(centred * centred, axis=-1, keepdims=True)
    normed = (centred * lax.rsqrt(variance + EPSILON)).astype(BF16)
    qkv_s[...] = mm(normed, wqkv_ref[...]).astype(BF16)

    def forward(g, _):
        at = pl.multiple_of(g * GROUP, GROUP)
        for b, (start, rows, _) in enumerate(BLOCKS):
            span = pl.ds(start, rows)
            q = qkv_s[span, pl.ds(at, GROUP)]
            k = qkv_s[span, pl.ds(inner + at, GROUP)]
            v = qkv_s[span, pl.ds(2 * inner + at, GROUP)]
            heads = range(PER_GROUP)
            scores = [mm_nt(q * masks[h], k) + bias_refs[b][...] for h in heads]
            tops = [jnp.max(s, axis=-1, keepdims=True) for s in scores]
            exps = [
                jnp.exp2((s - top) * (scale * 1.4426950408889634)) for s, top in zip(scores, tops)
            ]
            probs = [e * (1.0 / jnp.sum(e, axis=-1, keepdims=True)) for e in exps]
            for h in heads:
                p_refs[b][g * PER_GROUP + h] = probs[h]
            total = sum(mm(probs[h].astype(BF16), v * masks[h]) for h in heads)
            mixed_s[span, pl.ds(at, GROUP)] = total.astype(BF16)
        return 0

    lax.fori_loop(0, groups, forward, 0)

    mixed = mixed_s[...]
    output = u + mm(mixed, proj_ref[...])
    logits = mm_nt(output.astype(BF16), headt_ref[...])
    row = lax.broadcasted_iota(jnp.int32, (ROWS, 1), 0)
    real = (row < LOW_CELLS) | ((row >= LOW_ROWS) & (row < LOW_ROWS + HIGH_CELLS))
    logit_grad = LOSS_SCALE * (jax.nn.sigmoid(logits) - target)
    logit_grad = jnp.where(real, logit_grad, 0.0)
    lg_ref[0] = logit_grad
    grad_low = output_grad_of(logit_grad, headt_ref).astype(BF16)
    mg_s[...] = mm_nt(grad_low, proj_ref[...]).astype(BF16)
    for start, rows, _ in BLOCKS:
        acc_p[...] += mm(grad_low[start : start + rows].T, mixed[start : start + rows])

    def backward(g, _):
        at = pl.multiple_of(g * GROUP, GROUP)
        sets = []
        for b, (start, rows, _) in enumerate(BLOCKS):
            span = pl.ds(start, rows)
            q = qkv_s[span, pl.ds(at, GROUP)]
            k = qkv_s[span, pl.ds(inner + at, GROUP)]
            v = qkv_s[span, pl.ds(2 * inner + at, GROUP)]
            mg = mg_s[span, pl.ds(at, GROUP)]
            q_t = q.T
            mg_t = mg.T
            sets.append((b, span, q, k, v.T, mg, q_t, mg_t))
        heads = range(PER_GROUP)
        grads = [[mm(t[5] * masks[h], t[4]) for h in heads] for t in sets]
        all_values = [
            [
                mm(t[7][h * HEAD : (h + 1) * HEAD], p_refs[t[0]][g * PER_GROUP + h].astype(BF16))
                for h in heads
            ]
            for t in sets
        ]
        for t, grad, value_parts in zip(sets, grads, all_values):
            b, span, q, k, _, mg, q_t, mg_t = t
            ps = [p_refs[b][g * PER_GROUP + h] for h in heads]
            alongs = [jnp.sum(grad[h] * ps[h], axis=-1, keepdims=True) for h in heads]
            lows = [(ps[h] * (grad[h] - alongs[h]) * scale).astype(BF16) for h in heads]
            query_grad = sum(mm(lows[h], k * masks[h]) for h in heads)
            key_parts = [mm(q_t[h * HEAD : (h + 1) * HEAD], lows[h]) for h in heads]
            d_ref[0, span, pl.ds(at, GROUP)] = query_grad.astype(BF16)
            key_t = jnp.concatenate(key_parts, axis=0).astype(BF16)
            value_t = jnp.concatenate(value_parts, axis=0).astype(BF16)
            d_ref[0, span, pl.ds(inner + at, GROUP)] = key_t.T
            d_ref[0, span, pl.ds(2 * inner + at, GROUP)] = value_t.T
        return 0

    lax.fori_loop(0, groups, backward, 0)

    for start, rows, _ in BLOCKS:
        span = slice(start, start + rows)
        acc_q[...] += mm(normed[span].T, d_ref[0, span, :])


def output_grad_of(logit_grad, headt_ref):
    head = headt_ref[...].astype(F32)
    return (
        logit_grad[:, 0:1] * head[0:1]
        + logit_grad[:, 1:2] * head[1:2]
        + logit_grad[:, 2:3] * head[2:3]
    )


def first_kernel(info, vol_ref, aff_ref, index_ref, *rest):
    weights, outs, acc_q, acc_p = rest[:3], rest[3:6], rest[6], rest[7]
    own, scratch = rest[8], rest[9:]
    acc_q[...] = jnp.zeros_like(acc_q)
    acc_p[...] = jnp.zeros_like(acc_p)

    @pl.when(info[0] != 0)
    def _():
        own[...] = jnp.zeros_like(own)
        xs = ys = list(range(MARGIN, MARGIN + WIN))
        sources = take_own(vol_ref, aff_ref, own, xs, ys)
        sources = jnp.concatenate([sources, jnp.zeros((8, sources.shape[1]), BF16)], axis=0)
        cells = gather_rows(index_ref[0], sources)
        window_terms(info, 0, cells, weights, outs, acc_q, acc_p, scratch)


def rest_kernel(info, vol_ref, aff_ref, side_ref, front_ref, corner_ref, index_ref, *rest):
    weights, in_q, in_p = rest[:3], rest[3], rest[4]
    outs, keep_ref, send_ref = rest[8:11], rest[11], rest[12]
    acc_q, acc_p, first_q, first_p, sems, cells, own = rest[13:20]
    scratch = rest[20:]
    loads = (
        pltpu.make_async_copy(in_q, first_q, sems.at[0]),
        pltpu.make_async_copy(in_p, first_p, sems.at[1]),
    )
    window = pl.program_id(0) + 1
    near = list(range(MARGIN, MARGIN + WIN))
    far = list(range(MARGIN + WIN, 2 * WIN))

    @pl.when(window == 1)
    def _():
        for load in loads:
            load.start()
        acc_q[...] = jnp.zeros_like(acc_q)
        acc_p[...] = jnp.zeros_like(acc_p)
        own[...] = jnp.zeros_like(own)

    @pl.when((window == 1) & (info[1] != 0))
    def _():
        sources = jnp.concatenate(
            [take_own(vol_ref, aff_ref, own, near, far), side_ref[0:160]], axis=0
        )
        cells[...] = gather_rows(index_ref[0], sources)

    @pl.when((window == 2) & (info[2] != 0))
    def _():
        sources = jnp.concatenate(
            [take_own(vol_ref, aff_ref, own, far, near), front_ref[0:208]], axis=0
        )
        cells[...] = gather_rows(index_ref[0], sources)

    @pl.when((window == 3) & (info[3] != 0))
    def _():
        sources = jnp.concatenate(
            [
                take_own(vol_ref, aff_ref, own, far, far),
                side_ref[144:240],
                front_ref[48:240],
                corner_ref[...],
            ],
            axis=0,
        )
        cells[...] = gather_rows(index_ref[0], sources)

    @pl.when(info[window] != 0)
    def _():
        window_terms(info, window, cells[...], weights, outs, acc_q, acc_p, scratch)

    @pl.when(window == 3)
    def _():
        inner = acc_p.shape[1]
        share = acc_p.shape[0] // 16
        core = info[6]
        for load in loads:
            load.wait()

        def one(i, _):
            mine = pl.ds(pl.multiple_of((i * 2 + core) * share, 16), share)
            other = pl.ds(pl.multiple_of((i * 2 + 1 - core) * share, 16), share)
            y, near = lax.div(i, 2), lax.rem(i, 2)
            for part in range(3):
                at = slice(part * inner, (part + 1) * inner)
                keep_ref[y, part, near] = acc_q[mine, at] + first_q[mine, at]
                send_ref[y, part, near] = (acc_q[other, at] + first_q[other, at]).astype(BF16)
            keep_ref[y, 3, near] = acc_p[mine, :] + first_p[mine, :]
            send_ref[y, 3, near] = (acc_p[other, :] + first_p[other, :]).astype(BF16)
            return 0

        lax.fori_loop(0, 8, one, 0)


def window_pieces(window):
    a, b = window // 2, window % 2
    x_near = OUTER if a else WIN
    y_near = OUTER if b else WIN
    x_at, y_at = MARGIN + a * WIN, MARGIN + b * WIN
    pieces = [(0, 0, x_near, 0, y_near, x_at, y_at)]
    if b:
        pieces.append((1, 0, x_near, y_near, WIN, a * WIN, 0))
    if a:
        pieces.append((2, x_near, WIN, 0, y_near, 0, b * WIN))
    if a and b:
        pieces.append((3, x_near, WIN, y_near, WIN, 0, 0))
    return pieces


def cell_kernel(windows, held, info, tok_ref, lg_ref, d_ref, wqkv_ref, headt_ref, index_ref, *rest):
    *targets, cell, sems = rest[held:]
    if held:
        targets = {0: targets[0], 2: targets[1]}
    step = pl.program_id(0)
    window = jnp.where(step == 0, windows[0], windows[1])

    @pl.when(info[window] == 0)
    def _():
        cell[step] = jnp.zeros_like(cell[step])

    @pl.when(info[window] != 0)
    def _():
        u = tok_ref[0].astype(F32)
        mean_row = jnp.mean(u, axis=-1, keepdims=True)
        centred = u - mean_row
        variance = jnp.mean(centred * centred, axis=-1, keepdims=True)
        inv_std = lax.rsqrt(variance + EPSILON)
        unit_rows = centred * inv_std
        normed_grad = mm_nt(d_ref[0], wqkv_ref[...])
        grad_mean = jnp.mean(normed_grad, axis=-1, keepdims=True)
        grad_along = jnp.mean(normed_grad * unit_rows, axis=-1, keepdims=True)
        output_grad = output_grad_of(lg_ref[0], headt_ref)
        cell_low = output_grad + inv_std * (normed_grad - grad_mean - unit_rows * grad_along)
        at = lax.broadcasted_iota(jnp.int32, (WIN * WIN * 8, ROWS), 0)
        chosen = jnp.where(index_ref[0:1, :] == at, 1.0, 0.0).astype(BF16)
        placed = mm(chosen, cell_low.astype(BF16))
        placed = placed.reshape(WIN * WIN, 8, placed.shape[1])[:, :WIN].astype(BF16)
        cell[step] = placed.reshape(WIN, WIN, WIN, placed.shape[2])

    def copies(j):
        made = []
        for n, (t, x0, x1, y0, y1, to_x, to_y) in enumerate(window_pieces(windows[j])):
            made.append(
                pltpu.make_async_copy(
                    cell.at[j, x0:x1, y0:y1],
                    targets[t].at[to_x : to_x + x1 - x0, to_y : to_y + y1 - y0],
                    sems.at[j, n],
                )
            )
        return made

    @pl.when(step == 0)
    def _():
        for copy in copies(0):
            copy.start()

    @pl.when(step == 1)
    def _():
        for copy in copies(1):
            copy.start()
        for copy in copies(0) + copies(1):
            copy.wait()


def whole(shape):
    return pl.BlockSpec(shape, lambda i, *_: (0,) * len(shape))


def by_window(shape, first):
    return pl.BlockSpec((1,) + shape, lambda i, *_: (i + first,) + (0,) * len(shape))


PARAMS = pltpu.CompilerParams(vmem_limit_bytes=56 * 1024 * 1024)


def kept_shapes(width, inner):
    return [((ROWS, width), BF16), ((ROWS, 3), F32), ((ROWS, 3 * inner), BF16)]


def work_shapes(inner, width):
    heads = inner // HEAD
    return [
        pltpu.VMEM((64, 8, width + GROUP), F32),
        pltpu.VMEM((ROWS, 3 * inner), BF16),
        pltpu.VMEM((ROWS, inner), BF16),
        pltpu.VMEM((ROWS, inner), BF16),
        pltpu.VMEM((heads, LOW_ROWS, LOW_ROWS), F32),
        pltpu.VMEM((heads, HIGH_ROWS, HIGH_ROWS), F32),
        pltpu.VMEM((LOW_ROWS, LOW_ROWS), F32),
        pltpu.VMEM((HIGH_ROWS, HIGH_ROWS), F32),
    ]


def run_first(info, vol, aff, weights):
    inner, width = weights[1].shape
    kept = kept_shapes(width, inner)
    terms = [(width, 3 * inner), (width, inner)]
    return pl.pallas_call(
        first_kernel,
        name="first_window",
        grid_spec=pltpu.PrefetchScalarGridSpec(
            num_scalar_prefetch=1,
            grid=(1,),
            in_specs=[
                whole(vol.shape),
                whole(aff.shape),
                pl.BlockSpec((1, 8, 3 * GROUP), lambda i, *_: (0, 0, 0)),
                *[whole(w.shape) for w in weights],
            ],
            out_specs=[by_window(s, 0) for s, _ in kept] + [whole(s) for s in terms],
            scratch_shapes=work_shapes(inner, width),
        ),
        out_shape=[jax.ShapeDtypeStruct((4,) + s, d) for s, d in kept]
        + [jax.ShapeDtypeStruct(s, F32) for s in terms],
        compiler_params=PARAMS,
    )(info, vol, aff, jnp.asarray(source_rows()), *weights)


def run_rest(info, vol, aff, rims, weights, terms, kept_values):
    inner, width = weights[1].shape
    share = width // 16
    kept = kept_shapes(width, inner)
    return pl.pallas_call(
        rest_kernel,
        name="rest_windows",
        grid_spec=pltpu.PrefetchScalarGridSpec(
            num_scalar_prefetch=1,
            grid=(3,),
            in_specs=[
                whole(vol.shape),
                whole(aff.shape),
                *[whole(r.shape) for r in rims],
                pl.BlockSpec((1, 8, 3 * GROUP), lambda i, *_: (i + 1, 0, 0)),
                *[whole(w.shape) for w in weights],
                *[pl.BlockSpec(memory_space=pl.ANY) for _ in (*terms, *kept)],
            ],
            out_specs=[by_window(s, 1) for s, _ in kept] + [whole((4, 4, 2, share, inner))] * 2,
            scratch_shapes=[
                *[pltpu.VMEM((width, n * inner), F32) for n in (3, 1, 3, 1)],
                pltpu.SemaphoreType.DMA((2,)),
                pltpu.VMEM((ROWS, width + GROUP), F32),
            ]
            + work_shapes(inner, width),
        ),
        out_shape=[jax.ShapeDtypeStruct((4,) + s, d) for s, d in kept]
        + [
            jax.ShapeDtypeStruct((4, 4, 2, share, inner), F32),
            jax.ShapeDtypeStruct((4, 4, 2, share, inner), BF16),
        ],
        input_output_aliases={12 + i: i for i in range(3)},
        compiler_params=PARAMS,
    )(info, vol, aff, *rims, jnp.asarray(source_rows()), *weights, *terms, *kept_values)


def run_cells(windows, info, kept, wqkv, head_t, size_x, size_y, held):
    width = kept[0].shape[2]
    rest_x, rest_y = size_x - MARGIN, size_y - MARGIN
    first, change = windows[0], windows[1] - windows[0]

    def turned(shape):
        return pl.BlockSpec(
            (1,) + shape, lambda i, *_: (first + change * i,) + (0,) * len(shape)
        )

    shapes = [
        (size_x, size_y, WIN, width),
        (rest_x, MARGIN, WIN, width),
        (MARGIN, rest_y, WIN, width),
        (MARGIN, MARGIN, WIN, width),
    ]
    if held:
        shapes = [h.shape for h in held]
    anywhere = pl.BlockSpec(memory_space=pl.ANY)
    kernel = functools.partial(cell_kernel, windows, len(held))
    return pl.pallas_call(
        kernel,
        name="cell_grads",
        grid_spec=pltpu.PrefetchScalarGridSpec(
            num_scalar_prefetch=1,
            grid=(2,),
            in_specs=[
                *[turned(k.shape[1:]) for k in kept],
                whole(wqkv.shape),
                whole(head_t.shape),
                whole((8, ROWS)),
                *[anywhere for _ in held],
            ],
            out_specs=[anywhere] * len(shapes),
            scratch_shapes=[
                pltpu.VMEM((2, WIN, WIN, WIN, width), BF16),
                pltpu.SemaphoreType.DMA((2, 4)),
            ],
        ),
        out_shape=[jax.ShapeDtypeStruct(s, BF16) for s in shapes],
        input_output_aliases={7 + i: i for i in range(len(held))},
        compiler_params=PARAMS,
    )(info, *kept, wqkv, head_t, jnp.asarray(grid_rows()), *held)


def shifted(block, axes, shifts, sizes):
    first, second = sizes
    route = []
    for i in range(first):
        for j in range(second):
            to = ((i + shifts[0]) % first) * second + (j + shifts[1]) % second
            route.append((i * second + j, to))
    return lax.ppermute(block, axes, route)


def rim_message(vol, aff, rows):
    flat = jnp.concatenate([vol, aff], axis=-1)
    flat = flat.reshape(-1, flat.shape[-1])
    return jnp.pad(flat, ((0, rows - flat.shape[0]), (0, 0)))


def outgoing(total, position):
    size = total.shape[0]
    parts = []
    for shift in range(1, size):
        to = lax.rem(position + shift, size)
        parts.append(lax.dynamic_index_in_dim(total, to, 0, keepdims=False).astype(BF16))
    return parts


def incoming(total, position, got):
    mine = lax.dynamic_index_in_dim(total, position, 0, keepdims=False)
    for part in got:
        mine = mine + part.astype(F32)
    return mine


def axis_shares(total, axis, position):
    size = total.shape[0]
    got = [
        lax.ppermute(part, axis, [(i, (i + shift + 1) % size) for i in range(size)])
        for shift, part in enumerate(outgoing(total, position))
    ]
    return incoming(total, position, got)


def exchanged(parts, routes):
    return [lax.ppermute(part, "ga", route) for part, route in zip(parts, routes)]


def gathered(part, position, size):
    result = jnp.zeros((size,) + part.shape, part.dtype)
    result = lax.dynamic_update_index_in_dim(result, part, position, 0)
    for shift in range(1, size):
        got = lax.ppermute(part, "gy", [(i, (i + shift) % size) for i in range(size)])
        source = lax.rem(position + size - shift, size)
        result = lax.dynamic_update_index_in_dim(result, got, source, 0)
    return result


def per_device(volume, affinity, window_dest, qkv_weight, proj_weight, head_weight):
    size_x, size_y = volume.shape[1], volume.shape[2]
    n_gy, n_gx, n_ga = lax.axis_size("gy"), lax.axis_size("gx"), lax.axis_size("ga")
    gy, gx, ga = lax.axis_index("gy"), lax.axis_index("gx"), lax.axis_index("ga")
    m = MARGIN
    vol = volume[0]
    aff = jnp.pad(affinity[0].transpose(1, 2, 3, 0), ((0, 0), (0, 0), (0, 0), (0, GROUP - 3)))
    sizes = (n_gy, n_gx)
    axes = ("gy", "gx")

    side = shifted(rim_message(vol[m:, :m], aff[m:, :m], RIM_ROWS), axes, (0, -1), sizes)
    front = shifted(rim_message(vol[:m, m:], aff[:m, m:], RIM_ROWS), axes, (-1, 0), sizes)
    corner = shifted(rim_message(vol[:m, :m], aff[:m, :m], CORNER_ROWS), axes, (-1, -1), sizes)

    slot = lax.iota(jnp.int32, 8)
    live = jnp.pad(window_dest.reshape(-1), (0, 4))
    info = jnp.where(slot < 4, live < n_ga, False)
    info = info | ((slot == 4) & (gy == n_gy - 1)) | ((slot == 5) & (gx == n_gx - 1))
    info = (info | ((slot >= 6) & (lax.rem(ga, 2) == 1))).astype(jnp.int32)
    head_t = head_weight.T
    weights = (qkv_weight, proj_weight, head_t)

    *kept, term_q, term_p = run_first(info, vol, aff, weights)
    *kept, keep, send = run_rest(
        info, vol, aff, (side, front, corner), weights, (term_q, term_p), kept
    )
    info, send = lax.optimization_barrier((info, send))
    (got,) = exchanged([send], [[(i, i ^ 1) for i in range(n_ga)]])
    main, back_side, back_front, back_corner = run_cells(
        (3, 1), info, kept, qkv_weight, head_t, size_x, size_y, ()
    )
    total = keep + got.astype(F32)
    along = lax.div(ga, 4)
    parts = outgoing(total, along)
    info, back_side, back_corner, parts = lax.optimization_barrier(
        (info, back_side, back_corner, parts)
    )
    got = exchanged(
        parts, [[(i, (i + 4 * s) % n_ga) for i in range(n_ga)] for s in range(1, 4)]
    )
    back_side = shifted(back_side, axes, (0, 1), sizes)
    main, back_front = run_cells(
        (2, 0), info, kept, qkv_weight, head_t, size_x, size_y, (main, back_front)
    )
    total, back_front = lax.optimization_barrier((total, back_front))
    total = incoming(total, along, got)
    total = axis_shares(total, "gy", gy)
    total, back_side = lax.optimization_barrier((total, back_side))
    near = lax.rem(lax.div(ga, 2), 2)
    parts = outgoing(total, near)
    got = exchanged(parts, [[(i, i ^ 2) for i in range(n_ga)]])
    back_front = shifted(back_front, axes, (1, 0), sizes)
    back_corner = shifted(back_corner, axes, (1, 1), sizes)
    total = incoming(total, near, got)
    low = total.astype(BF16)
    for shift in range(1, n_gx):
        route = [(i, (i + shift) % n_gx) for i in range(n_gx)]
        total = total + lax.ppermute(low, "gx", route).astype(F32)
    total, back_front, back_corner = lax.optimization_barrier((total, back_front, back_corner))
    main = lax.dynamic_update_slice(main, back_side, (m, 0, 0, 0))
    main = lax.dynamic_update_slice(main, back_front, (0, m, 0, 0))
    main = lax.dynamic_update_slice(main, back_corner, (0, 0, 0, 0))
    total = total * (float(n_gy * n_gx * n_ga * 2 * WIN**3) ** (-0.5))
    parts = gathered(total, gy, n_gy)
    grad_qkv = jnp.concatenate([parts[0], parts[1], parts[2]], axis=1)
    return (main[None], grad_qkv, parts[3].T)


def solution(mesh):
    placed = (
        P("ga", "gy", "gx", None, None),
        P("ga", None, "gy", "gx", None),
        P("ga", "gy", "gx", None),
        P(),
        P(),
        P(),
    )
    return jax.shard_map(
        per_device,
        mesh=mesh,
        in_specs=placed,
        out_specs=(P("ga", "gy", "gx", None, None), P("ga", None), P(None, "ga")),
        check_vma=False,
    )
```

time: 550 us -> 145 us (0.26); the launches traced: 543 us -> 145 us
  waiting for transfers between devices: 327 us -> 22.9 us
  matrix products: 124 us -> 0 us
  Pallas kernels: 0 us -> 50.8 us
  starting transfers between devices: 27 us -> 55.1 us
  local copies, waits for them, and re-layouts: 30.1 us -> 11.7 us
  other arithmetic: 19.4 us -> 3.03 us
  between operations: 14.5 us -> 1.01 us
    psum x1 -> x0, waiting for transfers between devices: 158 us -> none  [per_device(): summed_qkv, summed_proj = lax.psum((share_qkv, share_proj), ('gy', 'gx'))]
    dot_general x38 -> x0, matrix products: 112 us -> none  [the longest x2 21.9 us: window_grads(): jnp.einsum('hqk,qhd->khd', score_low, queries, preferred_element_type=jnp...]
    reduce_scatter x2 -> x0, waiting for transfers between devices: 83.3 us -> none  [the longest x1 72.3 us: per_device(): lax.psum_scatter(total_qkv, 'ga', scatter_dimension=0, tiled=True)]
    ppermute x14 -> x20, waiting for transfers between devices: 85 us -> 22.9 us  [the longest x6 9.58 us: shifted(): return lax.ppermute(block, axes, route)]
    pallas_call x0 -> x4, Pallas kernels: none -> 50.8 us  [the longest x1 20.8 us: run_rest(): pl.pallas_call(rest_kernel, name='rest_windows', grid_spec=pltpu.Prefetch...]
    ppermute x14 -> x20, starting transfers between devices: 26.9 us -> 55.1 us  [the longest x6 26.2 us: shifted(): return lax.ppermute(block, axes, route)]
    sub x2 -> x0, matrix products: 12.3 us -> none  [window_grads(): exponent = jnp.exp(scores - row_max)]
    reshape x6 -> x3, local copies, waits for them, and re-layouts: 9.19 us -> 0.32 us  [rim_message(): flat = flat.reshape(-1, flat.shape[-1])]
  transfers between devices with their start and end apart: 17 -> 20, of which waited for: 11 -> 8; matrix products, arithmetic and copies ran while one was open for 8% -> 6% of each run, Pallas kernels for 0% -> 21%
where the time goes in v1:
time: 145 us
  starting transfers between devices  55.1 us (38%)
  Pallas kernels  50.8 us (35%)
  waiting for transfers between devices  22.9 us (16%)
  local copies, waits for them, and re-layouts  11.7 us (8%)
  other arithmetic  3.03 us (2%)
    ppermute x6, starting transfers between devices, shifted(): return lax.ppermute(block, axes, route)  26.2 us
    pallas_call x1, Pallas kernels, run_rest(): pl.pallas_call(rest_kernel, name='rest_windows', grid_spec=pltpu.Prefetch...  20.8 us
    pallas_call x1, Pallas kernels, run_first(): pl.pallas_call(first_kernel, name='first_window', grid_spec=pltpu.Prefetc...  17.6 us
    ppermute x5, starting transfers between devices, exchanged(): lax.ppermute(part, 'ga', route)  14.6 us
    pallas_call x2, Pallas kernels, run_cells(): pl.pallas_call(kernel, name='cell_grads', grid_spec=pltpu.PrefetchScalarG...  12.4 us
    ppermute x6, waiting for transfers between devices, shifted(): return lax.ppermute(block, axes, route)  9.58 us
    ppermute x3, starting transfers between devices, per_device(): total = total + lax.ppermute(low, 'gx', route).astype(F32)  7.21 us
    ppermute x3, starting transfers between devices, gathered(): lax.ppermute(part, 'gy', [(i, (i + shift) % size) for i in range(size)])  5.06 us
  transfers between devices with their start and end apart: 20, of which 8 were waited for; matrix products, arithmetic and copies ran while one was open for 6% of the time, Pallas kernels for 21%

profile of v1, /device:TPU:2, one launch (start us, length us, event | category | flops | bytes accessed | tf_op | source)
XLA Modules:
  0.0 144.7 jit_solution(2955750863913684373)
XLA Ops:
  0.6 1.7 %copy.18 = bf16[1,3,14,14,7]{1,4,3,2,0:T(8,128)(2,1)S(1)} copy(bf16[1,3,14,14,7]{3,4,2,1,0:T(8,128)(2,1)} %param.11) | data formatting | bytes 16464 | tf_op args[1]
  2.4 1.0 slice.40
  3.4 0.1 pad_maximum_fusion
  3.5 0.1 reshape.32
  3.7 6.4 %collective-permute-start = (bf16[240,896]{1,0:T(8,128)(2,1)S(1)}, bf16[240,896]{1,0:T(8,128)(2,1)S(1)}, u32[]{:S(2)}, u32[]{:S(2)}) collective-permute-start(bf16[240,896]{1,0:T(8,128)(2,1)S(1)} %pad.21), channel_id=1, source_target_pairs={{0,48},{16,0},{32,16},{48,32},{64,112},{80,64},{96,80},{112,96},{1... | collective-permute-start | bytes 1290248 | tf_op jit(solution)/shard_map/ppermute | solution.py:542
  10.1 1.0 slice.41
  11.2 0.0 copy-start.5
  11.2 0.1 pad_maximum_fusion.1
  11.3 0.1 reshape.33
  11.5 0.6 collective-permute-start.1
  12.1 0.9 slice.42
  13.1 3.7 %collective-permute-start.2 = (bf16[64,896]{1,0:T(8,128)(2,1)S(1)}, bf16[64,896]{1,0:T(8,128)(2,1)S(1)}, u32[]{:S(2)}, u32[]{:S(2)}) collective-permute-start(bf16[64,896]{1,0:T(8,128)(2,1)S(1)} %pad.23), channel_id=1, source_target_pairs={{0,240},{16,192},{32,208},{48,224},{64,48},{80,0},{96,16},{112,32}... | collective-permute-start | bytes 344072 | tf_op jit(solution)/shard_map/ppermute | solution.py:542
  16.8 0.9 pad.20.aff_ref
  17.7 0.5 or_convert_fusion.info
  18.2 17.6 %first_window.1 = (bf16[4,368,768]{2,1,0:T(8,128)(2,1)}, f32[4,368,3]{2,1,0:T(8,128)}, bf16[4,368,1152]{2,1,0:T(8,128)(2,1)}, f32[768,1152]{1,0:T(8,128)}, f32[768,384]{1,0:T(8,128)}) custom-call(s32[8]{0:T(128)} %or_convert_fusion.info, bf16[14,14,7,768]{3,2,1,0:T(8,128)(2,1)} %bitcast.66, bf16[14,14,7,128]{3,2,1,0:T(8,128)(2,1)} %pad.20.aff_ref, ...), custom_call_target="tpu_custom_call" | custom-call | tf_op jit(solution)/shard_map/first_window/pallas_call | solution.py:433
  35.8 0.0 collective-permute-done.2.corner_ref
  35.9 0.0 collective-permute-done.side_ref
  35.9 0.0 collective-permute-done.1.front_ref
  35.9 0.6 copy-done.4
  36.5 0.2 copy-done.1
  36.7 0.1 copy-done.2
  36.8 20.8 %rest_windows.1 = (bf16[4,368,768]{2,1,0:T(8,128)(2,1)}, f32[4,368,3]{2,1,0:T(8,128)}, bf16[4,368,1152]{2,1,0:T(8,128)(2,1)}, f32[4,4,2,48,384]{4,3,2,1,0:T(8,128)}, bf16[4,4,2,48,384]{4,3,2,1,0:T(8,128)(2,1)}) custom-call(s32[8]{0:T(128)} %or_convert_fusion.info, ...), custom_call_target="tpu_custom_call", output_to_operand_aliasing={{0}: (12, {}), {1}: (13, {}), {2}: (14, {})} | custom-call | tf_op jit(solution)/shard_map/rest_windows/pallas_call | solution.py:458
  57.6 0.1 collective-permute-start.3
  57.8 6.2 %cell_grads.2 = (bf16[14,14,7,768]{3,2,1,0:T(8,128)(2,1)}, bf16[11,3,7,768]{3,2,1,0:T(8,128)(2,1)}, bf16[3,11,7,768]{3,2,1,0:T(8,128)(2,1)}, bf16[3,3,7,768]{3,2,1,0:T(8,128)(2,1)}) custom-call(s32[8]{0:T(128)} %or_convert_fusion.info, bf16[4,368,768]{2,1,0:T(8,128)(2,1)} %get-tuple-element.41.tok_ref, f32[4,368,3]{2,1,0:T(8,128)} %get-tuple-element.42.lg_ref, ...), custom_call_target="tpu_custom_call" | custom-call | tf_op jit(solution)/shard_map/cell_grads/pallas_call | solution.py:510
  63.9 0.0 collective-permute-done.3
  63.9 0.3 convert_add_fusion
  64.2 0.8 fusion.4
  65.0 8.0 %collective-permute-start.4 = (bf16[4,2,48,384]{3,2,1,0:T(8,128)(2,1)}, bf16[4,2,48,384]{3,2,1,0:T(8,128)(2,1)}, u32[]{:S(2)}, u32[]{:S(2)}) collective-permute-start(bf16[4,2,48,384]{3,2,1,0:T(8,128)(2,1)} %get-tuple-element.54), channel_id=1, source_target_pairs={{0,4},{1,5},{2,6},{3,7},{4,8},{5,9},{6,10},{7,11},{8,12},{9,13},{1... | collective-permute-start | bytes 884744 | tf_op jit(solution)/shard_map/ppermute | solution.py:577
  73.0 5.8 %collective-permute-start.5 = (bf16[4,2,48,384]{3,2,1,0:T(8,128)(2,1)S(1)}, bf16[4,2,48,384]{3,2,1,0:T(8,128)(2,1)}, u32[]{:S(2)}, u32[]{:S(2)}) collective-permute-start(bf16[4,2,48,384]{3,2,1,0:T(8,128)(2,1)S(1)} %get-tuple-element.55), channel_id=1, source_target_pairs={{0,8},{1,9},{2,10},{3,11},{4,12},{5,13},{6,14},{7,15},{8,0},{9,1},... | collective-permute-start | bytes 884744 | tf_op jit(solution)/shard_map/ppermute | solution.py:577
  78.8 0.0 collective-permute-start.6
  78.8 6.2 %cell_grads.3 = (bf16[14,14,7,768]{3,2,1,0:T(8,128)(2,1)}, bf16[3,11,7,768]{3,2,1,0:T(8,128)(2,1)}) custom-call(s32[8]{0:T(128)} %or_convert_fusion.info, bf16[4,368,768]{2,1,0:T(8,128)(2,1)} %get-tuple-element.41.tok_ref, f32[4,368,3]{2,1,0:T(8,128)} %get-tuple-element.42.lg_ref, ...), custom_call_target="tpu_custom_call", output_to_operand_aliasing={{0}: (7, {}), {1}: (8, {})} | custom-call | tf_op jit(solution)/shard_map/cell_grads/pallas_call | solution.py:510
  85.0 0.0 copy-start.6
  85.0 15.4 %collective-permute-start.10 = (bf16[11,3,7,768]{3,2,1,0:T(8,128)(2,1)}, bf16[11,3,7,768]{3,2,1,0:T(8,128)(2,1)}, u32[]{:S(2)}, u32[]{:S(2)}) collective-permute-start(bf16[11,3,7,768]{3,2,1,0:T(8,128)(2,1)} %get-tuple-element.57), channel_id=1, source_target_pairs={{0,16},{16,32},{32,48},{48,0},{64,80},{80,96},{96,112},{112,64},{1... | collective-permute-start | bytes 1064456 | tf_op jit(solution)/shard_map/ppermute | solution.py:542
  100.4 0.0 collective-permute-done.4
  100.4 0.0 collective-permute-done.5
  100.4 0.0 collective-permute-done.6
  100.4 1.3 fusion.1
  101.8 0.1 collective-permute-start.7
  101.8 0.1 collective-permute-start.8
  101.9 1.9 %collective-permute-start.9 = (bf16[2,48,384]{2,1,0:T(8,128)(2,1)S(1)}, bf16[2,48,384]{2,1,0:T(8,128)(2,1)S(1)}, u32[]{:S(2)}, u32[]{:S(2)}) collective-permute-start(bf16[2,48,384]{2,1,0:T(8,128)(2,1)S(1)} %get-tuple-element.69), channel_id=1, source_target_pairs={{0,192},{64,0},{128,64},{192,128},{1,193},{65,1},{129,65},{193,129... | collective-permute-start | bytes 221192 | tf_op jit(solution)/shard_map/ppermute | solution.py:570
  103.9 2.5 %collective-permute-done.7 = bf16[2,48,384]{2,1,0:T(8,128)(2,1)S(1)} collective-permute-done((bf16[2,48,384]{2,1,0:T(8,128)(2,1)S(1)}, bf16[2,48,384]{2,1,0:T(8,128)(2,1)S(1)}, u32[]{:S(2)}, u32[]{:S(2)}) %collective-permute-start.7) | collective-permute-done | bytes 73760 | tf_op jit(solution)/shard_map/ppermute | solution.py:570
  106.3 1.7 %collective-permute-done.8 = bf16[2,48,384]{2,1,0:T(8,128)(2,1)S(1)} collective-permute-done((bf16[2,48,384]{2,1,0:T(8,128)(2,1)S(1)}, bf16[2,48,384]{2,1,0:T(8,128)(2,1)S(1)}, u32[]{:S(2)}, u32[]{:S(2)}) %collective-permute-start.8) | collective-permute-done | bytes 73760 | tf_op jit(solution)/shard_map/ppermute | solution.py:570
  108.0 0.4 collective-permute-done.9
  108.5 9.6 %collective-permute-done.10 = bf16[11,3,7,768]{3,2,1,0:T(8,128)(2,1)} collective-permute-done((bf16[11,3,7,768]{3,2,1,0:T(8,128)(2,1)}, bf16[11,3,7,768]{3,2,1,0:T(8,128)(2,1)}, u32[]{:S(2)}, u32[]{:S(2)}) %collective-permute-start.10) | collective-permute-done | bytes 354848 | tf_op jit(solution)/shard_map/ppermute | solution.py:542
  118.1 0.8 collective-permute-start.11
  118.8 0.0 collective-permute-start.15
  118.8 0.1 collective-permute-start.16
  118.9 3.1 %collective-permute-done.11 = bf16[48,384]{1,0:T(8,128)(2,1)S(1)} collective-permute-done((bf16[48,384]{1,0:T(8,128)(2,1)S(1)}, bf16[48,384]{1,0:T(8,128)(2,1)S(1)}, u32[]{:S(2)}, u32[]{:S(2)}) %collective-permute-start.11) | collective-permute-done | bytes 36896 | tf_op jit(solution)/shard_map/ppermute | solution.py:577
  122.0 3.5 %collective-permute-start.12 = (bf16[48,384]{1,0:T(8,128)(2,1)S(1)}, bf16[48,384]{1,0:T(8,128)(2,1)S(1)}, u32[]{:S(2)}, u32[]{:S(2)}) collective-permute-start(bf16[48,384]{1,0:T(8,128)(2,1)S(1)} %fusion.10), channel_id=1, source_target_pairs={{0,16},{16,32},{32,48},{48,0},{1,17},{17,33},{33,49},{49,1},{2,18}... | collective-permute-start | bytes 110600 | tf_op jit(solution)/shard_map/ppermute | solution.py:647
  125.6 0.0 collective-permute-start.13
  125.6 3.6 %collective-permute-start.14 = (bf16[48,384]{1,0:T(8,128)(2,1)S(1)}, bf16[48,384]{1,0:T(8,128)(2,1)S(1)}, u32[]{:S(2)}, u32[]{:S(2)}) collective-permute-start(bf16[48,384]{1,0:T(8,128)(2,1)S(1)} %fusion.10), channel_id=1, source_target_pairs={{0,48},{16,0},{32,16},{48,32},{1,49},{17,1},{33,17},{49,33},{2,50}... | collective-permute-start | bytes 110600 | tf_op jit(solution)/shard_map/ppermute | solution.py:647
  129.2 1.8 %bitcast_dynamic-update-slice_fusion.1 = bf16[1,14,14,7,768]{4,3,2,1,0:T(8,128)(2,1)} fusion(bf16[1,14,14,7,768]{4,3,2,1,0:T(8,128)(2,1)} %bitcast.72, bf16[11,3,7,768]{3,2,1,0:T(8,128)(2,1)} %collective-permute-done.10), kind=kLoop, calls=%fused_computation.10 | loop fusion | bytes 811008 | tf_op jit(solution)/shard_map/dynamic_update_slice | solution.py:649
  131.0 0.0 collective-permute-done.12
  131.0 2.8 %collective-permute-done.13 = bf16[48,384]{1,0:T(8,128)(2,1)S(1)} collective-permute-done((bf16[48,384]{1,0:T(8,128)(2,1)S(1)}, bf16[48,384]{1,0:T(8,128)(2,1)S(1)}, u32[]{:S(2)}, u32[]{:S(2)}) %collective-permute-start.13) | collective-permute-done | bytes 36896 | tf_op jit(solution)/shard_map/ppermute | solution.py:647
  133.8 0.0 collective-permute-done.14
  133.9 0.0 collective-permute-done.16
  133.9 2.0 %collective-permute-start.17 = (f32[48,384]{1,0:T(8,128)S(1)}, f32[48,384]{1,0:T(8,128)S(1)}, u32[]{:S(2)}, u32[]{:S(2)}) collective-permute-start(f32[48,384]{1,0:T(8,128)S(1)} %broadcast_multiply_fusion), channel_id=1, source_target_pairs={{0,64},{64,128},{128,192},{192,0},{1,65},{65,129},{129,193},{193,1... | collective-permute-start | bytes 221192 | tf_op jit(solution)/shard_map/ppermute | solution.py:584
  135.9 3.1 %collective-permute-start.18 = (f32[48,384]{1,0:T(8,128)S(1)}, f32[48,384]{1,0:T(8,128)S(1)}, u32[]{:S(2)}, u32[]{:S(2)}) collective-permute-start(f32[48,384]{1,0:T(8,128)S(1)} %broadcast_multiply_fusion), channel_id=1, source_target_pairs={{0,128},{64,192},{128,0},{192,64},{1,129},{65,193},{129,1},{193,65... | collective-permute-start | bytes 221192 | tf_op jit(solution)/shard_map/ppermute | solution.py:584
  139.0 0.8 bitcast_dynamic-update-slice_fusion
  139.7 0.7 bitcast_dynamic-update-slice_fusion.2
  140.5 1.3 collective-permute-done.18
  141.7 1.6 %collective-permute-done.19 = f32[48,384]{1,0:T(8,128)S(1)} collective-permute-done((f32[48,384]{1,0:T(8,128)S(1)}, f32[48,384]{1,0:T(8,128)S(1)}, u32[]{:S(2)}, u32[]{:S(2)}) %collective-permute-start.19) | collective-permute-done | bytes 73760 | tf_op jit(solution)/shard_map/ppermute | solution.py:584
  143.3 0.7 slice_bitcast_fusion
  144.0 0.7 pad_maximum_fusion.2
  (31 shorter events, 0.4 us)
Async XLA Ops:
  3.7 32.1 %collective-permute-start = (bf16[240,896]{1,0:T(8,128)(2,1)S(1)}, bf16[240,896]{1,0:T(8,128)(2,1)S(1)}, u32[]{:S(2)}, u32[]{:S(2)}) collective-permute-start(bf16[240,896]{1,0:T(8,128)(2,1)S(1)} %pad.21), channel_id=1, source_target_pairs={{0,48},{16,0},{32,16},{48,32},{64,112},{80,64},{96,80},{112,96},{1... | collective-permute-start | bytes 1290248 | tf_op jit(solution)/shard_map/ppermute | solution.py:542
  11.2 6.5 %copy-start.5 = (s32[1,1,1,4]{3,2,1,0:T(1,128)S(1)}, s32[1,1,1,4]{3,2,1,0:T(1,128)}, u32[]{:S(2)}) copy-start(s32[1,1,1,4]{3,2,1,0:T(1,128)} %param.12) | copy-start | bytes 52
  11.5 24.4 %collective-permute-start.1 = (bf16[240,896]{1,0:T(8,128)(2,1)S(1)}, bf16[240,896]{1,0:T(8,128)(2,1)S(1)}, u32[]{:S(2)}, u32[]{:S(2)}) collective-permute-start(bf16[240,896]{1,0:T(8,128)(2,1)S(1)} %pad.22), channel_id=1, source_target_pairs={{0,192},{16,208},{32,224},{48,240},{64,0},{80,16},{96,32},{112,48}... | collective-permute-start | bytes 1290248 | tf_op jit(solution)/shard_map/ppermute | solution.py:542
  13.1 22.8 %collective-permute-start.2 = (bf16[64,896]{1,0:T(8,128)(2,1)S(1)}, bf16[64,896]{1,0:T(8,128)(2,1)S(1)}, u32[]{:S(2)}, u32[]{:S(2)}) collective-permute-start(bf16[64,896]{1,0:T(8,128)(2,1)S(1)} %pad.23), channel_id=1, source_target_pairs={{0,240},{16,192},{32,208},{48,224},{64,48},{80,0},{96,16},{112,32}... | collective-permute-start | bytes 344072 | tf_op jit(solution)/shard_map/ppermute | solution.py:542
  35.8 0.6 copy-start.4
  35.9 0.8 copy-start.1
  35.9 0.9 copy-start.2
  57.6 6.3 %collective-permute-start.3 = (bf16[4,4,2,48,384]{4,3,2,1,0:T(8,128)(2,1)}, bf16[4,4,2,48,384]{4,3,2,1,0:T(8,128)(2,1)S(1)}, u32[]{:S(2)}, u32[]{:S(2)}) collective-permute-start(bf16[4,4,2,48,384]{4,3,2,1,0:T(8,128)(2,1)} %get-tuple-element.47), channel_id=1, source_target_pairs={{0,1},{1,0},{2,3},{3,2},{4,5},{5,4},{6,7},{7,6},{8,9},{9,8},{10,11... | collective-permute-start | bytes 3538952 | tf_op jit(solution)/shard_map/ppermute | solution.py:577
  57.8 6.2 %copy-start = (f32[4,4,2,48,384]{4,3,2,1,0:T(8,128)S(1)}, f32[4,4,2,48,384]{4,3,2,1,0:T(8,128)}, u32[]{:S(2)}) copy-start(f32[4,4,2,48,384]{4,3,2,1,0:T(8,128)} %get-tuple-element.46) | copy-start | bytes 7077892
  65.0 35.4 %collective-permute-start.4 = (bf16[4,2,48,384]{3,2,1,0:T(8,128)(2,1)}, bf16[4,2,48,384]{3,2,1,0:T(8,128)(2,1)}, u32[]{:S(2)}, u32[]{:S(2)}) collective-permute-start(bf16[4,2,48,384]{3,2,1,0:T(8,128)(2,1)} %get-tuple-element.54), channel_id=1, source_target_pairs={{0,4},{1,5},{2,6},{3,7},{4,8},{5,9},{6,10},{7,11},{8,12},{9,13},{1... | collective-permute-start | bytes 884744 | tf_op jit(solution)/shard_map/ppermute | solution.py:577
  73.0 27.4 %collective-permute-start.5 = (bf16[4,2,48,384]{3,2,1,0:T(8,128)(2,1)S(1)}, bf16[4,2,48,384]{3,2,1,0:T(8,128)(2,1)}, u32[]{:S(2)}, u32[]{:S(2)}) collective-permute-start(bf16[4,2,48,384]{3,2,1,0:T(8,128)(2,1)S(1)} %get-tuple-element.55), channel_id=1, source_target_pairs={{0,8},{1,9},{2,10},{3,11},{4,12},{5,13},{6,14},{7,15},{8,0},{9,1},... | collective-permute-start | bytes 884744 | tf_op jit(solution)/shard_map/ppermute | solution.py:577
  78.8 21.7 %collective-permute-start.6 = (bf16[4,2,48,384]{3,2,1,0:T(8,128)(2,1)S(1)}, bf16[4,2,48,384]{3,2,1,0:T(8,128)(2,1)}, u32[]{:S(2)}, u32[]{:S(2)}) collective-permute-start(bf16[4,2,48,384]{3,2,1,0:T(8,128)(2,1)S(1)} %get-tuple-element.56), channel_id=1, source_target_pairs={{0,12},{1,13},{2,14},{3,15},{4,0},{5,1},{6,2},{7,3},{8,4},{9,5},{1... | collective-permute-start | bytes 884744 | tf_op jit(solution)/shard_map/ppermute | solution.py:577
  85.0 33.8 %copy-start.3 = (bf16[3,11,7,768]{3,2,1,0:T(8,128)(2,1)S(1)}, bf16[3,11,7,768]{3,2,1,0:T(8,128)(2,1)}, u32[]{:S(2)}) copy-start(bf16[3,11,7,768]{3,2,1,0:T(8,128)(2,1)} %get-tuple-element.60) | copy-start | bytes 1064452
  85.0 33.8 %copy-start.6 = (bf16[3,3,7,768]{3,2,1,0:T(8,128)(2,1)S(1)}, bf16[3,3,7,768]{3,2,1,0:T(8,128)(2,1)}, u32[]{:S(2)}) copy-start(bf16[3,3,7,768]{3,2,1,0:T(8,128)(2,1)} %get-tuple-element.61) | copy-start | bytes 290308
  85.0 33.0 %collective-permute-start.10 = (bf16[11,3,7,768]{3,2,1,0:T(8,128)(2,1)}, bf16[11,3,7,768]{3,2,1,0:T(8,128)(2,1)}, u32[]{:S(2)}, u32[]{:S(2)}) collective-permute-start(bf16[11,3,7,768]{3,2,1,0:T(8,128)(2,1)} %get-tuple-element.57), channel_id=1, source_target_pairs={{0,16},{16,32},{32,48},{48,0},{64,80},{80,96},{96,112},{112,64},{1... | collective-permute-start | bytes 1064456 | tf_op jit(solution)/shard_map/ppermute | solution.py:542
  101.8 4.6 %collective-permute-start.7 = (bf16[2,48,384]{2,1,0:T(8,128)(2,1)S(1)}, bf16[2,48,384]{2,1,0:T(8,128)(2,1)S(1)}, u32[]{:S(2)}, u32[]{:S(2)}) collective-permute-start(bf16[2,48,384]{2,1,0:T(8,128)(2,1)S(1)} %get-tuple-element.68), channel_id=1, source_target_pairs={{0,64},{64,128},{128,192},{192,0},{1,65},{65,129},{129,193},{193,1... | collective-permute-start | bytes 221192 | tf_op jit(solution)/shard_map/ppermute | solution.py:570
  101.8 6.2 %collective-permute-start.8 = (bf16[2,48,384]{2,1,0:T(8,128)(2,1)S(1)}, bf16[2,48,384]{2,1,0:T(8,128)(2,1)S(1)}, u32[]{:S(2)}, u32[]{:S(2)}) collective-permute-start(bf16[2,48,384]{2,1,0:T(8,128)(2,1)S(1)} %get-tuple-element.70), channel_id=1, source_target_pairs={{0,128},{64,192},{128,0},{192,64},{1,129},{65,193},{129,1},{193,65... | collective-permute-start | bytes 221192 | tf_op jit(solution)/shard_map/ppermute | solution.py:570
  101.9 6.5 %collective-permute-start.9 = (bf16[2,48,384]{2,1,0:T(8,128)(2,1)S(1)}, bf16[2,48,384]{2,1,0:T(8,128)(2,1)S(1)}, u32[]{:S(2)}, u32[]{:S(2)}) collective-permute-start(bf16[2,48,384]{2,1,0:T(8,128)(2,1)S(1)} %get-tuple-element.69), channel_id=1, source_target_pairs={{0,192},{64,0},{128,64},{192,128},{1,193},{65,1},{129,65},{193,129... | collective-permute-start | bytes 221192 | tf_op jit(solution)/shard_map/ppermute | solution.py:570
  118.1 4.0 %collective-permute-start.11 = (bf16[48,384]{1,0:T(8,128)(2,1)S(1)}, bf16[48,384]{1,0:T(8,128)(2,1)S(1)}, u32[]{:S(2)}, u32[]{:S(2)}) collective-permute-start(bf16[48,384]{1,0:T(8,128)(2,1)S(1)} %fusion.11), channel_id=1, source_target_pairs={{0,2},{1,3},{2,0},{3,1},{4,6},{5,7},{6,4},{7,5},{8,10},{9,11},{10,... | collective-permute-start | bytes 110600 | tf_op jit(solution)/shard_map/ppermute | solution.py:577
  118.8 15.0 %collective-permute-start.15 = (bf16[3,11,7,768]{3,2,1,0:T(8,128)(2,1)S(1)}, bf16[3,11,7,768]{3,2,1,0:T(8,128)(2,1)S(1)}, u32[]{:S(2)}, u32[]{:S(2)}) collective-permute-start(bf16[3,11,7,768]{3,2,1,0:T(8,128)(2,1)S(1)} %copy-done.3), channel_id=1, source_target_pairs={{0,64},{16,80},{32,96},{48,112},{64,128},{80,144},{96,160},{112,17... | collective-permute-start | bytes 1064456 | tf_op jit(solution)/shard_map/ppermute | solution.py:542
  118.8 15.0 %collective-permute-start.16 = (bf16[3,3,7,768]{3,2,1,0:T(8,128)(2,1)S(1)}, bf16[3,3,7,768]{3,2,1,0:T(8,128)(2,1)S(1)}, u32[]{:S(2)}, u32[]{:S(2)}) collective-permute-start(bf16[3,3,7,768]{3,2,1,0:T(8,128)(2,1)S(1)} %copy-done.6), channel_id=1, source_target_pairs={{0,80},{16,96},{32,112},{48,64},{64,144},{80,160},{96,176},{112,12... | collective-permute-start | bytes 290312 | tf_op jit(solution)/shard_map/ppermute | solution.py:542
  122.0 9.0 %collective-permute-start.12 = (bf16[48,384]{1,0:T(8,128)(2,1)S(1)}, bf16[48,384]{1,0:T(8,128)(2,1)S(1)}, u32[]{:S(2)}, u32[]{:S(2)}) collective-permute-start(bf16[48,384]{1,0:T(8,128)(2,1)S(1)} %fusion.10), channel_id=1, source_target_pairs={{0,16},{16,32},{32,48},{48,0},{1,17},{17,33},{33,49},{49,1},{2,18}... | collective-permute-start | bytes 110600 | tf_op jit(solution)/shard_map/ppermute | solution.py:647
  125.6 8.3 %collective-permute-start.13 = (bf16[48,384]{1,0:T(8,128)(2,1)S(1)}, bf16[48,384]{1,0:T(8,128)(2,1)S(1)}, u32[]{:S(2)}, u32[]{:S(2)}) collective-permute-start(bf16[48,384]{1,0:T(8,128)(2,1)S(1)} %fusion.10), channel_id=1, source_target_pairs={{0,32},{16,48},{32,0},{48,16},{1,33},{17,49},{33,1},{49,17},{2,34}... | collective-permute-start | bytes 110600 | tf_op jit(solution)/shard_map/ppermute | solution.py:647
  125.6 8.2 %collective-permute-start.14 = (bf16[48,384]{1,0:T(8,128)(2,1)S(1)}, bf16[48,384]{1,0:T(8,128)(2,1)S(1)}, u32[]{:S(2)}, u32[]{:S(2)}) collective-permute-start(bf16[48,384]{1,0:T(8,128)(2,1)S(1)} %fusion.10), channel_id=1, source_target_pairs={{0,48},{16,0},{32,16},{48,32},{1,49},{17,1},{33,17},{49,33},{2,50}... | collective-permute-start | bytes 110600 | tf_op jit(solution)/shard_map/ppermute | solution.py:647
  133.9 6.5 %collective-permute-start.17 = (f32[48,384]{1,0:T(8,128)S(1)}, f32[48,384]{1,0:T(8,128)S(1)}, u32[]{:S(2)}, u32[]{:S(2)}) collective-permute-start(f32[48,384]{1,0:T(8,128)S(1)} %broadcast_multiply_fusion), channel_id=1, source_target_pairs={{0,64},{64,128},{128,192},{192,0},{1,65},{65,129},{129,193},{193,1... | collective-permute-start | bytes 221192 | tf_op jit(solution)/shard_map/ppermute | solution.py:584
  135.9 5.9 %collective-permute-start.18 = (f32[48,384]{1,0:T(8,128)S(1)}, f32[48,384]{1,0:T(8,128)S(1)}, u32[]{:S(2)}, u32[]{:S(2)}) collective-permute-start(f32[48,384]{1,0:T(8,128)S(1)} %broadcast_multiply_fusion), channel_id=1, source_target_pairs={{0,128},{64,192},{128,0},{192,64},{1,129},{65,193},{129,1},{193,65... | collective-permute-start | bytes 221192 | tf_op jit(solution)/shard_map/ppermute | solution.py:584
  138.9 4.4 %collective-permute-start.19 = (f32[48,384]{1,0:T(8,128)S(1)}, f32[48,384]{1,0:T(8,128)S(1)}, u32[]{:S(2)}, u32[]{:S(2)}) collective-permute-start(f32[48,384]{1,0:T(8,128)S(1)} %broadcast_multiply_fusion), channel_id=1, source_target_pairs={{0,192},{64,0},{128,64},{192,128},{1,193},{65,1},{129,65},{193,129... | collective-permute-start | bytes 221192 | tf_op jit(solution)/shard_map/ppermute | solution.py:584

commit v2 on v1

--- a/solution.py
+++ b/solution.py
@@ -124,7 +124,7 @@
     return mm(chosen, sources)
 
 
-def window_terms(info, window, cells, weights, outs, acc_q, acc_p, scratch):
+def window_terms(info, window, cells, weights, outs, acc_q, acc_p, scratch, fresh):
     wqkv_ref, proj_ref, headt_ref = weights
     tok_ref, lg_ref, d_ref = outs
     qkv_s, mixed_s, mg_s, p_low, p_high, bias_low, bias_high = scratch
@@ -183,7 +183,8 @@
     grad_low = output_grad_of(logit_grad, headt_ref).astype(BF16)
     mg_s[...] = mm_nt(grad_low, proj_ref[...]).astype(BF16)
     for start, rows, _ in BLOCKS:
-        acc_p[...] += mm(grad_low[start : start + rows].T, mixed[start : start + rows])
+        term = mm(grad_low[start : start + rows].T, mixed[start : start + rows])
+        acc_p[...] = term if fresh and start == 0 else acc_p[...] + term
 
     def backward(g, _):
         at = pl.multiple_of(g * GROUP, GROUP)
@@ -224,7 +225,8 @@
 
     for start, rows, _ in BLOCKS:
         span = slice(start, start + rows)
-        acc_q[...] += mm(normed[span].T, d_ref[0, span, :])
+        term = mm(normed[span].T, d_ref[0, span, :])
+        acc_q[...] = term if fresh and start == 0 else acc_q[...] + term
 
 
 def output_grad_of(logit_grad, headt_ref):
@@ -239,8 +241,11 @@
 def first_kernel(info, vol_ref, aff_ref, index_ref, *rest):
     weights, outs, acc_q, acc_p = rest[:3], rest[3:6], rest[6], rest[7]
     own, scratch = rest[8], rest[9:]
-    acc_q[...] = jnp.zeros_like(acc_q)
-    acc_p[...] = jnp.zeros_like(acc_p)
+
+    @pl.when(info[0] == 0)
+    def _():
+        acc_q[...] = jnp.zeros_like(acc_q)
+        acc_p[...] = jnp.zeros_like(acc_p)
 
     @pl.when(info[0] != 0)
     def _():
@@ -249,7 +254,7 @@
         sources = take_own(vol_ref, aff_ref, own, xs, ys)
         sources = jnp.concatenate([sources, jnp.zeros((8, sources.shape[1]), BF16)], axis=0)
         cells = gather_rows(index_ref[0], sources)
-        window_terms(info, 0, cells, weights, outs, acc_q, acc_p, scratch)
+        window_terms(info, 0, cells, weights, outs, acc_q, acc_p, scratch, True)
 
 
 def rest_kernel(info, vol_ref, aff_ref, side_ref, front_ref, corner_ref, index_ref, *rest):
@@ -302,7 +307,7 @@
 
     @pl.when(info[window] != 0)
     def _():
-        window_terms(info, window, cells[...], weights, outs, acc_q, acc_p, scratch)
+        window_terms(info, window, cells[...], weights, outs, acc_q, acc_p, scratch, False)
 
     @pl.when(window == 3)
     def _():

time: 145 us -> 145 us (level)
  no operation moved by 1% of the time
where the time goes in v2:
time: 145 us; the launch traced here: 144 us
  starting transfers between devices  55.5 us (38%)
  Pallas kernels  50.5 us (35%)
  waiting for transfers between devices  22.6 us (16%)
  local copies, waits for them, and re-layouts  11.7 us (8%)
  other arithmetic  3.03 us (2%)
    ppermute x6, starting transfers between devices, shifted(): return lax.ppermute(block, axes, route)  25.9 us
    pallas_call x1, Pallas kernels, run_rest(): pl.pallas_call(rest_kernel, name='rest_windows', grid_spec=pltpu.Prefetch...  20.8 us
    pallas_call x1, Pallas kernels, run_first(): pl.pallas_call(first_kernel, name='first_window', grid_spec=pltpu.Prefetc...  17.3 us
    ppermute x5, starting transfers between devices, exchanged(): lax.ppermute(part, 'ga', route)  15.2 us
    pallas_call x2, Pallas kernels, run_cells(): pl.pallas_call(kernel, name='cell_grads', grid_spec=pltpu.PrefetchScalarG...  12.4 us
    ppermute x6, waiting for transfers between devices, shifted(): return lax.ppermute(block, axes, route)  9.58 us
    ppermute x3, starting transfers between devices, per_device(): total = total + lax.ppermute(low, 'gx', route).astype(F32)  7.22 us
    ppermute x3, starting transfers between devices, gathered(): lax.ppermute(part, 'gy', [(i, (i + shift) % size) for i in range(size)])  5.07 us
  transfers between devices with their start and end apart: 20, of which 8 were waited for; matrix products, arithmetic and copies ran while one was open for 6% of the time, Pallas kernels for 21%

profile of v2, /device:TPU:2, one launch (start us, length us, event | category | flops | bytes accessed | tf_op | source)
XLA Modules:
  0.0 144.4 jit_solution(15821331697425437006)
XLA Ops:
  0.6 1.7 %copy.18 = bf16[1,3,14,14,7]{1,4,3,2,0:T(8,128)(2,1)S(1)} copy(bf16[1,3,14,14,7]{3,4,2,1,0:T(8,128)(2,1)} %param.11) | data formatting | bytes 16464 | tf_op args[1]
  2.4 1.0 slice.40
  3.4 0.1 pad_maximum_fusion
  3.5 0.1 reshape.32
  3.7 6.4 %collective-permute-start = (bf16[240,896]{1,0:T(8,128)(2,1)S(1)}, bf16[240,896]{1,0:T(8,128)(2,1)S(1)}, u32[]{:S(2)}, u32[]{:S(2)}) collective-permute-start(bf16[240,896]{1,0:T(8,128)(2,1)S(1)} %pad.21), channel_id=1, source_target_pairs={{0,48},{16,0},{32,16},{48,32},{64,112},{80,64},{96,80},{112,96},{1... | collective-permute-start | bytes 1290248 | tf_op jit(solution)/shard_map/ppermute | solution.py:547
  10.1 1.0 slice.41
  11.2 0.0 copy-start.5
  11.2 0.1 pad_maximum_fusion.1
  11.3 0.1 reshape.33
  11.5 0.6 collective-permute-start.1
  12.1 0.9 slice.42
  13.1 3.7 %collective-permute-start.2 = (bf16[64,896]{1,0:T(8,128)(2,1)S(1)}, bf16[64,896]{1,0:T(8,128)(2,1)S(1)}, u32[]{:S(2)}, u32[]{:S(2)}) collective-permute-start(bf16[64,896]{1,0:T(8,128)(2,1)S(1)} %pad.23), channel_id=1, source_target_pairs={{0,240},{16,192},{32,208},{48,224},{64,48},{80,0},{96,16},{112,32}... | collective-permute-start | bytes 344072 | tf_op jit(solution)/shard_map/ppermute | solution.py:547
  16.8 0.9 pad.20.aff_ref
  17.7 0.5 or_convert_fusion.info
  18.2 17.3 %first_window.1 = (bf16[4,368,768]{2,1,0:T(8,128)(2,1)}, f32[4,368,3]{2,1,0:T(8,128)}, bf16[4,368,1152]{2,1,0:T(8,128)(2,1)}, f32[768,1152]{1,0:T(8,128)}, f32[768,384]{1,0:T(8,128)}) custom-call(s32[8]{0:T(128)} %or_convert_fusion.info, bf16[14,14,7,768]{3,2,1,0:T(8,128)(2,1)} %bitcast.66, bf16[14,14,7,128]{3,2,1,0:T(8,128)(2,1)} %pad.20.aff_ref, ...), custom_call_target="tpu_custom_call" | custom-call | tf_op jit(solution)/shard_map/first_window/pallas_call | solution.py:438
  35.5 0.0 collective-permute-done.2.corner_ref
  35.5 0.0 collective-permute-done.side_ref
  35.6 0.0 collective-permute-done.1.front_ref
  35.6 0.6 copy-done.4
  36.2 0.2 copy-done.1
  36.4 0.1 copy-done.2
  36.5 20.8 %rest_windows.1 = (bf16[4,368,768]{2,1,0:T(8,128)(2,1)}, f32[4,368,3]{2,1,0:T(8,128)}, bf16[4,368,1152]{2,1,0:T(8,128)(2,1)}, f32[4,4,2,48,384]{4,3,2,1,0:T(8,128)}, bf16[4,4,2,48,384]{4,3,2,1,0:T(8,128)(2,1)}) custom-call(s32[8]{0:T(128)} %or_convert_fusion.info, ...), custom_call_target="tpu_custom_call", output_to_operand_aliasing={{0}: (12, {}), {1}: (13, {}), {2}: (14, {})} | custom-call | tf_op jit(solution)/shard_map/rest_windows/pallas_call | solution.py:463
  57.3 0.1 collective-permute-start.3
  57.5 6.2 %cell_grads.2 = (bf16[14,14,7,768]{3,2,1,0:T(8,128)(2,1)}, bf16[11,3,7,768]{3,2,1,0:T(8,128)(2,1)}, bf16[3,11,7,768]{3,2,1,0:T(8,128)(2,1)}, bf16[3,3,7,768]{3,2,1,0:T(8,128)(2,1)}) custom-call(s32[8]{0:T(128)} %or_convert_fusion.info, bf16[4,368,768]{2,1,0:T(8,128)(2,1)} %get-tuple-element.41.tok_ref, f32[4,368,3]{2,1,0:T(8,128)} %get-tuple-element.42.lg_ref, ...), custom_call_target="tpu_custom_call" | custom-call | tf_op jit(solution)/shard_map/cell_grads/pallas_call | solution.py:515
  63.6 0.0 collective-permute-done.3
  63.6 0.3 convert_add_fusion
  63.9 0.8 fusion.4
  64.7 8.3 %collective-permute-start.4 = (bf16[4,2,48,384]{3,2,1,0:T(8,128)(2,1)}, bf16[4,2,48,384]{3,2,1,0:T(8,128)(2,1)}, u32[]{:S(2)}, u32[]{:S(2)}) collective-permute-start(bf16[4,2,48,384]{3,2,1,0:T(8,128)(2,1)} %get-tuple-element.54), channel_id=1, source_target_pairs={{0,4},{1,5},{2,6},{3,7},{4,8},{5,9},{6,10},{7,11},{8,12},{9,13},{1... | collective-permute-start | bytes 884744 | tf_op jit(solution)/shard_map/ppermute | solution.py:582
  73.0 5.8 %collective-permute-start.5 = (bf16[4,2,48,384]{3,2,1,0:T(8,128)(2,1)S(1)}, bf16[4,2,48,384]{3,2,1,0:T(8,128)(2,1)}, u32[]{:S(2)}, u32[]{:S(2)}) collective-permute-start(bf16[4,2,48,384]{3,2,1,0:T(8,128)(2,1)S(1)} %get-tuple-element.55), channel_id=1, source_target_pairs={{0,8},{1,9},{2,10},{3,11},{4,12},{5,13},{6,14},{7,15},{8,0},{9,1},... | collective-permute-start | bytes 884744 | tf_op jit(solution)/shard_map/ppermute | solution.py:582
  78.8 0.0 collective-permute-start.6
  78.8 6.2 %cell_grads.3 = (bf16[14,14,7,768]{3,2,1,0:T(8,128)(2,1)}, bf16[3,11,7,768]{3,2,1,0:T(8,128)(2,1)}) custom-call(s32[8]{0:T(128)} %or_convert_fusion.info, bf16[4,368,768]{2,1,0:T(8,128)(2,1)} %get-tuple-element.41.tok_ref, f32[4,368,3]{2,1,0:T(8,128)} %get-tuple-element.42.lg_ref, ...), custom_call_target="tpu_custom_call", output_to_operand_aliasing={{0}: (7, {}), {1}: (8, {})} | custom-call | tf_op jit(solution)/shard_map/cell_grads/pallas_call | solution.py:515
  85.0 0.0 copy-start.6
  85.0 15.1 %collective-permute-start.10 = (bf16[11,3,7,768]{3,2,1,0:T(8,128)(2,1)}, bf16[11,3,7,768]{3,2,1,0:T(8,128)(2,1)}, u32[]{:S(2)}, u32[]{:S(2)}) collective-permute-start(bf16[11,3,7,768]{3,2,1,0:T(8,128)(2,1)} %get-tuple-element.57), channel_id=1, source_target_pairs={{0,16},{16,32},{32,48},{48,0},{64,80},{80,96},{96,112},{112,64},{1... | collective-permute-start | bytes 1064456 | tf_op jit(solution)/shard_map/ppermute | solution.py:547
  100.1 0.0 collective-permute-done.4
  100.1 0.0 collective-permute-done.5
  100.1 0.0 collective-permute-done.6
  100.1 1.3 fusion.1
  101.4 0.1 collective-permute-start.7
  101.5 0.1 collective-permute-start.8
  101.6 1.9 %collective-permute-start.9 = (bf16[2,48,384]{2,1,0:T(8,128)(2,1)S(1)}, bf16[2,48,384]{2,1,0:T(8,128)(2,1)S(1)}, u32[]{:S(2)}, u32[]{:S(2)}) collective-permute-start(bf16[2,48,384]{2,1,0:T(8,128)(2,1)S(1)} %get-tuple-element.69), channel_id=1, source_target_pairs={{0,192},{64,0},{128,64},{192,128},{1,193},{65,1},{129,65},{193,129... | collective-permute-start | bytes 221192 | tf_op jit(solution)/shard_map/ppermute | solution.py:575
  103.5 2.5 %collective-permute-done.7 = bf16[2,48,384]{2,1,0:T(8,128)(2,1)S(1)} collective-permute-done((bf16[2,48,384]{2,1,0:T(8,128)(2,1)S(1)}, bf16[2,48,384]{2,1,0:T(8,128)(2,1)S(1)}, u32[]{:S(2)}, u32[]{:S(2)}) %collective-permute-start.7) | collective-permute-done | bytes 73760 | tf_op jit(solution)/shard_map/ppermute | solution.py:575
  106.0 1.7 %collective-permute-done.8 = bf16[2,48,384]{2,1,0:T(8,128)(2,1)S(1)} collective-permute-done((bf16[2,48,384]{2,1,0:T(8,128)(2,1)S(1)}, bf16[2,48,384]{2,1,0:T(8,128)(2,1)S(1)}, u32[]{:S(2)}, u32[]{:S(2)}) %collective-permute-start.8) | collective-permute-done | bytes 73760 | tf_op jit(solution)/shard_map/ppermute | solution.py:575
  107.7 0.4 collective-permute-done.9
  108.2 9.6 %collective-permute-done.10 = bf16[11,3,7,768]{3,2,1,0:T(8,128)(2,1)} collective-permute-done((bf16[11,3,7,768]{3,2,1,0:T(8,128)(2,1)}, bf16[11,3,7,768]{3,2,1,0:T(8,128)(2,1)}, u32[]{:S(2)}, u32[]{:S(2)}) %collective-permute-start.10) | collective-permute-done | bytes 354848 | tf_op jit(solution)/shard_map/ppermute | solution.py:547
  117.7 1.1 collective-permute-start.11
  118.8 0.0 collective-permute-start.15
  118.8 0.1 collective-permute-start.16
  118.9 2.8 %collective-permute-done.11 = bf16[48,384]{1,0:T(8,128)(2,1)S(1)} collective-permute-done((bf16[48,384]{1,0:T(8,128)(2,1)S(1)}, bf16[48,384]{1,0:T(8,128)(2,1)S(1)}, u32[]{:S(2)}, u32[]{:S(2)}) %collective-permute-start.11) | collective-permute-done | bytes 36896 | tf_op jit(solution)/shard_map/ppermute | solution.py:582
  121.7 3.5 %collective-permute-start.12 = (bf16[48,384]{1,0:T(8,128)(2,1)S(1)}, bf16[48,384]{1,0:T(8,128)(2,1)S(1)}, u32[]{:S(2)}, u32[]{:S(2)}) collective-permute-start(bf16[48,384]{1,0:T(8,128)(2,1)S(1)} %fusion.10), channel_id=1, source_target_pairs={{0,16},{16,32},{32,48},{48,0},{1,17},{17,33},{33,49},{49,1},{2,18}... | collective-permute-start | bytes 110600 | tf_op jit(solution)/shard_map/ppermute | solution.py:652
  125.3 0.0 collective-permute-start.13
  125.3 3.7 %collective-permute-start.14 = (bf16[48,384]{1,0:T(8,128)(2,1)S(1)}, bf16[48,384]{1,0:T(8,128)(2,1)S(1)}, u32[]{:S(2)}, u32[]{:S(2)}) collective-permute-start(bf16[48,384]{1,0:T(8,128)(2,1)S(1)} %fusion.10), channel_id=1, source_target_pairs={{0,48},{16,0},{32,16},{48,32},{1,49},{17,1},{33,17},{49,33},{2,50}... | collective-permute-start | bytes 110600 | tf_op jit(solution)/shard_map/ppermute | solution.py:652
  128.9 1.8 %bitcast_dynamic-update-slice_fusion.1 = bf16[1,14,14,7,768]{4,3,2,1,0:T(8,128)(2,1)} fusion(bf16[1,14,14,7,768]{4,3,2,1,0:T(8,128)(2,1)} %bitcast.72, bf16[11,3,7,768]{3,2,1,0:T(8,128)(2,1)} %collective-permute-done.10), kind=kLoop, calls=%fused_computation.10 | loop fusion | bytes 811008 | tf_op jit(solution)/shard_map/dynamic_update_slice | solution.py:654
  130.7 2.8 %collective-permute-done.13 = bf16[48,384]{1,0:T(8,128)(2,1)S(1)} collective-permute-done((bf16[48,384]{1,0:T(8,128)(2,1)S(1)}, bf16[48,384]{1,0:T(8,128)(2,1)S(1)}, u32[]{:S(2)}, u32[]{:S(2)}) %collective-permute-start.13) | collective-permute-done | bytes 36896 | tf_op jit(solution)/shard_map/ppermute | solution.py:652
  133.5 0.0 collective-permute-done.16
  133.6 2.0 %collective-permute-start.17 = (f32[48,384]{1,0:T(8,128)S(1)}, f32[48,384]{1,0:T(8,128)S(1)}, u32[]{:S(2)}, u32[]{:S(2)}) collective-permute-start(f32[48,384]{1,0:T(8,128)S(1)} %broadcast_multiply_fusion), channel_id=1, source_target_pairs={{0,64},{64,128},{128,192},{192,0},{1,65},{65,129},{129,193},{193,1... | collective-permute-start | bytes 221192 | tf_op jit(solution)/shard_map/ppermute | solution.py:589
  135.6 3.1 %collective-permute-start.18 = (f32[48,384]{1,0:T(8,128)S(1)}, f32[48,384]{1,0:T(8,128)S(1)}, u32[]{:S(2)}, u32[]{:S(2)}) collective-permute-start(f32[48,384]{1,0:T(8,128)S(1)} %broadcast_multiply_fusion), channel_id=1, source_target_pairs={{0,128},{64,192},{128,0},{192,64},{1,129},{65,193},{129,1},{193,65... | collective-permute-start | bytes 221192 | tf_op jit(solution)/shard_map/ppermute | solution.py:589
  138.7 0.0 collective-permute-start.19
  138.7 0.8 bitcast_dynamic-update-slice_fusion
  139.4 0.7 bitcast_dynamic-update-slice_fusion.2
  140.1 0.0 collective-permute-done.17
  140.2 1.3 collective-permute-done.18
  141.4 1.6 %collective-permute-done.19 = f32[48,384]{1,0:T(8,128)S(1)} collective-permute-done((f32[48,384]{1,0:T(8,128)S(1)}, f32[48,384]{1,0:T(8,128)S(1)}, u32[]{:S(2)}, u32[]{:S(2)}) %collective-permute-start.19) | collective-permute-done | bytes 73760 | tf_op jit(solution)/shard_map/ppermute | solution.py:589
  143.0 0.7 slice_bitcast_fusion
  143.7 0.7 pad_maximum_fusion.2
  (31 shorter events, 0.4 us)
Async XLA Ops:
  3.7 31.8 %collective-permute-start = (bf16[240,896]{1,0:T(8,128)(2,1)S(1)}, bf16[240,896]{1,0:T(8,128)(2,1)S(1)}, u32[]{:S(2)}, u32[]{:S(2)}) collective-permute-start(bf16[240,896]{1,0:T(8,128)(2,1)S(1)} %pad.21), channel_id=1, source_target_pairs={{0,48},{16,0},{32,16},{48,32},{64,112},{80,64},{96,80},{112,96},{1... | collective-permute-start | bytes 1290248 | tf_op jit(solution)/shard_map/ppermute | solution.py:547
  11.2 6.5 %copy-start.5 = (s32[1,1,1,4]{3,2,1,0:T(1,128)S(1)}, s32[1,1,1,4]{3,2,1,0:T(1,128)}, u32[]{:S(2)}) copy-start(s32[1,1,1,4]{3,2,1,0:T(1,128)} %param.12) | copy-start | bytes 52
  11.5 24.1 %collective-permute-start.1 = (bf16[240,896]{1,0:T(8,128)(2,1)S(1)}, bf16[240,896]{1,0:T(8,128)(2,1)S(1)}, u32[]{:S(2)}, u32[]{:S(2)}) collective-permute-start(bf16[240,896]{1,0:T(8,128)(2,1)S(1)} %pad.22), channel_id=1, source_target_pairs={{0,192},{16,208},{32,224},{48,240},{64,0},{80,16},{96,32},{112,48}... | collective-permute-start | bytes 1290248 | tf_op jit(solution)/shard_map/ppermute | solution.py:547
  13.1 22.4 %collective-permute-start.2 = (bf16[64,896]{1,0:T(8,128)(2,1)S(1)}, bf16[64,896]{1,0:T(8,128)(2,1)S(1)}, u32[]{:S(2)}, u32[]{:S(2)}) collective-permute-start(bf16[64,896]{1,0:T(8,128)(2,1)S(1)} %pad.23), channel_id=1, source_target_pairs={{0,240},{16,192},{32,208},{48,224},{64,48},{80,0},{96,16},{112,32}... | collective-permute-start | bytes 344072 | tf_op jit(solution)/shard_map/ppermute | solution.py:547
  35.5 0.6 copy-start.4
  35.6 0.8 copy-start.1
  35.6 0.9 copy-start.2
  57.3 6.3 %collective-permute-start.3 = (bf16[4,4,2,48,384]{4,3,2,1,0:T(8,128)(2,1)}, bf16[4,4,2,48,384]{4,3,2,1,0:T(8,128)(2,1)S(1)}, u32[]{:S(2)}, u32[]{:S(2)}) collective-permute-start(bf16[4,4,2,48,384]{4,3,2,1,0:T(8,128)(2,1)} %get-tuple-element.47), channel_id=1, source_target_pairs={{0,1},{1,0},{2,3},{3,2},{4,5},{5,4},{6,7},{7,6},{8,9},{9,8},{10,11... | collective-permute-start | bytes 3538952 | tf_op jit(solution)/shard_map/ppermute | solution.py:582
  57.4 6.2 %copy-start = (f32[4,4,2,48,384]{4,3,2,1,0:T(8,128)S(1)}, f32[4,4,2,48,384]{4,3,2,1,0:T(8,128)}, u32[]{:S(2)}) copy-start(f32[4,4,2,48,384]{4,3,2,1,0:T(8,128)} %get-tuple-element.46) | copy-start | bytes 7077892
  64.7 35.4 %collective-permute-start.4 = (bf16[4,2,48,384]{3,2,1,0:T(8,128)(2,1)}, bf16[4,2,48,384]{3,2,1,0:T(8,128)(2,1)}, u32[]{:S(2)}, u32[]{:S(2)}) collective-permute-start(bf16[4,2,48,384]{3,2,1,0:T(8,128)(2,1)} %get-tuple-element.54), channel_id=1, source_target_pairs={{0,4},{1,5},{2,6},{3,7},{4,8},{5,9},{6,10},{7,11},{8,12},{9,13},{1... | collective-permute-start | bytes 884744 | tf_op jit(solution)/shard_map/ppermute | solution.py:582
  73.0 27.1 %collective-permute-start.5 = (bf16[4,2,48,384]{3,2,1,0:T(8,128)(2,1)S(1)}, bf16[4,2,48,384]{3,2,1,0:T(8,128)(2,1)}, u32[]{:S(2)}, u32[]{:S(2)}) collective-permute-start(bf16[4,2,48,384]{3,2,1,0:T(8,128)(2,1)S(1)} %get-tuple-element.55), channel_id=1, source_target_pairs={{0,8},{1,9},{2,10},{3,11},{4,12},{5,13},{6,14},{7,15},{8,0},{9,1},... | collective-permute-start | bytes 884744 | tf_op jit(solution)/shard_map/ppermute | solution.py:582
  78.8 21.4 %collective-permute-start.6 = (bf16[4,2,48,384]{3,2,1,0:T(8,128)(2,1)S(1)}, bf16[4,2,48,384]{3,2,1,0:T(8,128)(2,1)}, u32[]{:S(2)}, u32[]{:S(2)}) collective-permute-start(bf16[4,2,48,384]{3,2,1,0:T(8,128)(2,1)S(1)} %get-tuple-element.56), channel_id=1, source_target_pairs={{0,12},{1,13},{2,14},{3,15},{4,0},{5,1},{6,2},{7,3},{8,4},{9,5},{1... | collective-permute-start | bytes 884744 | tf_op jit(solution)/shard_map/ppermute | solution.py:582
  85.0 33.8 %copy-start.3 = (bf16[3,11,7,768]{3,2,1,0:T(8,128)(2,1)S(1)}, bf16[3,11,7,768]{3,2,1,0:T(8,128)(2,1)}, u32[]{:S(2)}) copy-start(bf16[3,11,7,768]{3,2,1,0:T(8,128)(2,1)} %get-tuple-element.60) | copy-start | bytes 1064452
  85.0 33.8 %copy-start.6 = (bf16[3,3,7,768]{3,2,1,0:T(8,128)(2,1)S(1)}, bf16[3,3,7,768]{3,2,1,0:T(8,128)(2,1)}, u32[]{:S(2)}) copy-start(bf16[3,3,7,768]{3,2,1,0:T(8,128)(2,1)} %get-tuple-element.61) | copy-start | bytes 290308
  85.0 32.7 %collective-permute-start.10 = (bf16[11,3,7,768]{3,2,1,0:T(8,128)(2,1)}, bf16[11,3,7,768]{3,2,1,0:T(8,128)(2,1)}, u32[]{:S(2)}, u32[]{:S(2)}) collective-permute-start(bf16[11,3,7,768]{3,2,1,0:T(8,128)(2,1)} %get-tuple-element.57), channel_id=1, source_target_pairs={{0,16},{16,32},{32,48},{48,0},{64,80},{80,96},{96,112},{112,64},{1... | collective-permute-start | bytes 1064456 | tf_op jit(solution)/shard_map/ppermute | solution.py:547
  101.4 4.6 %collective-permute-start.7 = (bf16[2,48,384]{2,1,0:T(8,128)(2,1)S(1)}, bf16[2,48,384]{2,1,0:T(8,128)(2,1)S(1)}, u32[]{:S(2)}, u32[]{:S(2)}) collective-permute-start(bf16[2,48,384]{2,1,0:T(8,128)(2,1)S(1)} %get-tuple-element.68), channel_id=1, source_target_pairs={{0,64},{64,128},{128,192},{192,0},{1,65},{65,129},{129,193},{193,1... | collective-permute-start | bytes 221192 | tf_op jit(solution)/shard_map/ppermute | solution.py:575
  101.5 6.2 %collective-permute-start.8 = (bf16[2,48,384]{2,1,0:T(8,128)(2,1)S(1)}, bf16[2,48,384]{2,1,0:T(8,128)(2,1)S(1)}, u32[]{:S(2)}, u32[]{:S(2)}) collective-permute-start(bf16[2,48,384]{2,1,0:T(8,128)(2,1)S(1)} %get-tuple-element.70), channel_id=1, source_target_pairs={{0,128},{64,192},{128,0},{192,64},{1,129},{65,193},{129,1},{193,65... | collective-permute-start | bytes 221192 | tf_op jit(solution)/shard_map/ppermute | solution.py:575
  101.6 6.5 %collective-permute-start.9 = (bf16[2,48,384]{2,1,0:T(8,128)(2,1)S(1)}, bf16[2,48,384]{2,1,0:T(8,128)(2,1)S(1)}, u32[]{:S(2)}, u32[]{:S(2)}) collective-permute-start(bf16[2,48,384]{2,1,0:T(8,128)(2,1)S(1)} %get-tuple-element.69), channel_id=1, source_target_pairs={{0,192},{64,0},{128,64},{192,128},{1,193},{65,1},{129,65},{193,129... | collective-permute-start | bytes 221192 | tf_op jit(solution)/shard_map/ppermute | solution.py:575
  117.7 4.0 %collective-permute-start.11 = (bf16[48,384]{1,0:T(8,128)(2,1)S(1)}, bf16[48,384]{1,0:T(8,128)(2,1)S(1)}, u32[]{:S(2)}, u32[]{:S(2)}) collective-permute-start(bf16[48,384]{1,0:T(8,128)(2,1)S(1)} %fusion.11), channel_id=1, source_target_pairs={{0,2},{1,3},{2,0},{3,1},{4,6},{5,7},{6,4},{7,5},{8,10},{9,11},{10,... | collective-permute-start | bytes 110600 | tf_op jit(solution)/shard_map/ppermute | solution.py:582
  118.8 14.7 %collective-permute-start.15 = (bf16[3,11,7,768]{3,2,1,0:T(8,128)(2,1)S(1)}, bf16[3,11,7,768]{3,2,1,0:T(8,128)(2,1)S(1)}, u32[]{:S(2)}, u32[]{:S(2)}) collective-permute-start(bf16[3,11,7,768]{3,2,1,0:T(8,128)(2,1)S(1)} %copy-done.3), channel_id=1, source_target_pairs={{0,64},{16,80},{32,96},{48,112},{64,128},{80,144},{96,160},{112,17... | collective-permute-start | bytes 1064456 | tf_op jit(solution)/shard_map/ppermute | solution.py:547
  118.8 14.7 %collective-permute-start.16 = (bf16[3,3,7,768]{3,2,1,0:T(8,128)(2,1)S(1)}, bf16[3,3,7,768]{3,2,1,0:T(8,128)(2,1)S(1)}, u32[]{:S(2)}, u32[]{:S(2)}) collective-permute-start(bf16[3,3,7,768]{3,2,1,0:T(8,128)(2,1)S(1)} %copy-done.6), channel_id=1, source_target_pairs={{0,80},{16,96},{32,112},{48,64},{64,144},{80,160},{96,176},{112,12... | collective-permute-start | bytes 290312 | tf_op jit(solution)/shard_map/ppermute | solution.py:547
  121.7 9.0 %collective-permute-start.12 = (bf16[48,384]{1,0:T(8,128)(2,1)S(1)}, bf16[48,384]{1,0:T(8,128)(2,1)S(1)}, u32[]{:S(2)}, u32[]{:S(2)}) collective-permute-start(bf16[48,384]{1,0:T(8,128)(2,1)S(1)} %fusion.10), channel_id=1, source_target_pairs={{0,16},{16,32},{32,48},{48,0},{1,17},{17,33},{33,49},{49,1},{2,18}... | collective-permute-start | bytes 110600 | tf_op jit(solution)/shard_map/ppermute | solution.py:652
  125.3 8.3 %collective-permute-start.13 = (bf16[48,384]{1,0:T(8,128)(2,1)S(1)}, bf16[48,384]{1,0:T(8,128)(2,1)S(1)}, u32[]{:S(2)}, u32[]{:S(2)}) collective-permute-start(bf16[48,384]{1,0:T(8,128)(2,1)S(1)} %fusion.10), channel_id=1, source_target_pairs={{0,32},{16,48},{32,0},{48,16},{1,33},{17,49},{33,1},{49,17},{2,34}... | collective-permute-start | bytes 110600 | tf_op jit(solution)/shard_map/ppermute | solution.py:652
  125.3 8.3 %collective-permute-start.14 = (bf16[48,384]{1,0:T(8,128)(2,1)S(1)}, bf16[48,384]{1,0:T(8,128)(2,1)S(1)}, u32[]{:S(2)}, u32[]{:S(2)}) collective-permute-start(bf16[48,384]{1,0:T(8,128)(2,1)S(1)} %fusion.10), channel_id=1, source_target_pairs={{0,48},{16,0},{32,16},{48,32},{1,49},{17,1},{33,17},{49,33},{2,50}... | collective-permute-start | bytes 110600 | tf_op jit(solution)/shard_map/ppermute | solution.py:652
  133.6 6.6 %collective-permute-start.17 = (f32[48,384]{1,0:T(8,128)S(1)}, f32[48,384]{1,0:T(8,128)S(1)}, u32[]{:S(2)}, u32[]{:S(2)}) collective-permute-start(f32[48,384]{1,0:T(8,128)S(1)} %broadcast_multiply_fusion), channel_id=1, source_target_pairs={{0,64},{64,128},{128,192},{192,0},{1,65},{65,129},{129,193},{193,1... | collective-permute-start | bytes 221192 | tf_op jit(solution)/shard_map/ppermute | solution.py:589
  135.6 5.9 %collective-permute-start.18 = (f32[48,384]{1,0:T(8,128)S(1)}, f32[48,384]{1,0:T(8,128)S(1)}, u32[]{:S(2)}, u32[]{:S(2)}) collective-permute-start(f32[48,384]{1,0:T(8,128)S(1)} %broadcast_multiply_fusion), channel_id=1, source_target_pairs={{0,128},{64,192},{128,0},{192,64},{1,129},{65,193},{129,1},{193,65... | collective-permute-start | bytes 221192 | tf_op jit(solution)/shard_map/ppermute | solution.py:589
  138.7 4.4 %collective-permute-start.19 = (f32[48,384]{1,0:T(8,128)S(1)}, f32[48,384]{1,0:T(8,128)S(1)}, u32[]{:S(2)}, u32[]{:S(2)}) collective-permute-start(f32[48,384]{1,0:T(8,128)S(1)} %broadcast_multiply_fusion), channel_id=1, source_target_pairs={{0,192},{64,0},{128,64},{192,128},{1,193},{65,1},{129,65},{193,129... | collective-permute-start | bytes 221192 | tf_op jit(solution)/shard_map/ppermute | solution.py:589
